TPU v7x, 32 devices: a whole 2x2x4 slice. The times are simulated.
32 devices in a mesh: dp: 8 (over z, x), tensor: 4 (over y, core).
Axes of the slice: x: 2, y: 2, z: 4, core: 2. Of those that a mesh axis runs over, the one named last changes fastest.
Arguments:
- tokens: bfloat16 [4096, 768], P(('dp', 'tensor')), may hold values from -6 to 6
- pair_features: bfloat16 [16, 256, 256, 256], P('dp', 'tensor'), may hold values from -6 to 6
- cotangent: bfloat16 [4096, 768], P(('dp', 'tensor')), may hold values from -6 to 6
- chain_length: int32 [16], P('dp'), may hold values from 64 to 256, as said below
- time_bin: int32 [16], P('dp'), may hold values from 0 to 63
- cath_class: int32 [16], P('dp'), may hold values from 0 to 63
- bias_weight: bfloat16 [256, 12], replicated, may hold values from -0.375 to 0.375
- input_weight: bfloat16 [3, 768, 768], P(None, None, 'tensor'), may hold values from -0.21875 to 0.21875
- output_weight: bfloat16 [768, 768], P('tensor'), may hold values from -0.875 to 0.875
- hidden_weight: bfloat16 [2, 768, 3072], P(None, None, 'tensor'), may hold values from -0.21875 to 0.21875
- down_weight: bfloat16 [3072, 768], P('tensor'), may hold values from -0.109375 to 0.109375
- modulation_weight: bfloat16 [256, 4608], replicated, may hold values from -0.375 to 0.375
- time_table: bfloat16 [64, 256], replicated, may hold values from -4 to 4
- class_table: bfloat16 [64, 256], replicated, may hold values from -4 to 4
Outputs:
- result: bfloat16 [4096, 768], P(('dp', 'tensor'))
- grad_tokens: bfloat16 [4096, 768], P(('dp', 'tensor'))
- grad_pair: bfloat16 [16, 256, 256, 256], P('dp', 'tensor')
- grad_bias_weight: float32 [256, 12], replicated
- grad_input_weight: float32 [3, 768, 768], P(None, 'dp', 'tensor')
- grad_output_weight: float32 [768, 768], P('tensor', 'dp')
- grad_hidden_weight: float32 [2, 768, 3072], P(None, 'dp', 'tensor')
- grad_down_weight: float32 [3072, 768], P('tensor', 'dp')
- grad_modulation_weight: float32 [256, 4608], replicated
- grad_time_table: float32 [64, 256], replicated
- grad_class_table: float32 [64, 256], replicated
Inputs may be any that keep to these rules, and one draw needn't show every extreme that they name: `chain_length`: every chain has at least 64 residues; the first chain slot of the whole batch is full.
All inputs are finite; a program needn't handle non-finite values.
Results may differ from a plain program's by a relative error of at most 0.02.
The roundings to bfloat16 on the way count: a program that leaves them out, or rounds other values in their place, can miss the bound.
Values may be sent and summed in bfloat16 or wider, within the bound.
A program may use at most 128 MiB of HBM per device.

v0:
```python
import jax
import jax.numpy as jnp
from jax import lax
from jax.sharding import PartitionSpec as P

HD = 64


HIGH = lax.Precision.HIGHEST
EPSILON = 1e-05


def layer_norm(row_block):
    centre = row_block - jnp.mean(row_block, axis=-1, keepdims=True)
    inverse = lax.rsqrt(jnp.mean(centre * centre, axis=-1, keepdims=True) + EPSILON)
    return (centre * inverse, inverse)


def norm_back(grad_norm, normed, inverse):
    return inverse * (
        grad_norm
        - jnp.mean(grad_norm, axis=-1, keepdims=True)
        - normed * jnp.mean(grad_norm * normed, axis=-1, keepdims=True)
    )


def scores_of(query_rows, key_rows, bias_full, keep_mask):
    raw_scores = jnp.einsum(
        "cqhd,ckhd->chqk", query_rows, key_rows, preferred_element_type=jnp.float32
    ) * HD ** (-0.5) + bias_full.astype(jnp.float32)
    return jnp.where(keep_mask[:, None, None, :], raw_scores, -1000000000.0)


def body(
    tokens,
    pair_features,
    cotangent,
    chain_length,
    time_bin,
    cath_class,
    bias_weight,
    input_weight,
    output_weight,
    hidden_weight,
    down_weight,
    modulation_weight,
    time_table,
    class_table,
):
    tensor_rank = lax.axis_index("tensor")
    chain_count = pair_features.shape[0]
    chain_span = pair_features.shape[2]
    local_rows = tokens.shape[0]
    model_width = tokens.shape[1]
    heads_local = input_weight.shape[2] // HD
    group_rows = chain_count * chain_span
    float_bf = jnp.bfloat16
    time_hot = (time_bin[:, None] == jnp.arange(time_table.shape[0])[None, :]).astype(jnp.float32)
    class_hot = (cath_class[:, None] == jnp.arange(class_table.shape[0])[None, :]).astype(
        jnp.float32
    )
    condition = jnp.dot(time_hot, time_table.astype(jnp.float32), precision=HIGH) + jnp.dot(
        class_hot, class_table.astype(jnp.float32), precision=HIGH
    )
    mod_weight = modulation_weight.astype(jnp.float32)
    modulation = jnp.dot(condition, mod_weight, precision=HIGH)
    row_index = tensor_rank * local_rows + jnp.arange(local_rows)
    row_chain = row_index // chain_span
    row_place = row_index % chain_span
    select = (row_chain[:, None] == jnp.arange(chain_count)[None, :]).astype(jnp.float32)
    row_mods = jnp.dot(select, modulation, precision=HIGH).reshape(local_rows, 6, model_width)
    row_limit = jnp.sum(jnp.where(select > 0, chain_length[None, :], 0), axis=1)
    row_mask = (row_place < row_limit).astype(jnp.float32)[:, None]
    keep_mask = jnp.arange(chain_span)[None, :] < chain_length[:, None]
    inputs = tokens.astype(jnp.float32)
    norm_attend, inverse_attend = layer_norm(inputs)
    h_attend = (norm_attend * (1.0 + row_mods[:, 0]) + row_mods[:, 1]).astype(float_bf)
    bias_local = jnp.einsum(
        "cijp,ph->chij", pair_features, bias_weight, preferred_element_type=jnp.float32
    ).astype(float_bf)
    bias_full = lax.all_to_all(bias_local, "tensor", split_axis=1, concat_axis=2, tiled=True)
    piece = lax.all_gather(h_attend, "tensor", axis=0, tiled=True)
    rows_attend = piece
    projected = jnp.einsum(
        "rd,tde->rte", piece, input_weight, preferred_element_type=jnp.float32
    ).astype(float_bf)
    query_rows = projected[:, 0].reshape(chain_count, chain_span, heads_local, HD)
    key_rows = projected[:, 1].reshape(chain_count, chain_span, heads_local, HD)
    value_rows = projected[:, 2].reshape(chain_count, chain_span, heads_local, HD)
    logits = scores_of(query_rows, key_rows, bias_full, keep_mask)
    row_top = jnp.max(logits, axis=-1, keepdims=True)
    log_total = row_top + jnp.log(jnp.sum(jnp.exp(logits - row_top), axis=-1, keepdims=True))
    soft_weights = jnp.exp(logits - log_total).astype(float_bf)
    attended = (
        jnp.einsum("chqk,ckhd->cqhd", soft_weights, value_rows, preferred_element_type=jnp.float32)
        .astype(float_bf)
        .reshape(group_rows, heads_local * HD)
    )
    out_attend = lax.psum_scatter(
        jnp.dot(attended, output_weight, preferred_element_type=jnp.float32),
        "tensor",
        scatter_dimension=0,
        tiled=True,
    )
    gate_attend = jax.nn.sigmoid(row_mods[:, 2])
    middle = inputs + row_mask * gate_attend * out_attend
    norm_hidden, inverse_hidden = layer_norm(middle)
    h_hidden = (norm_hidden * (1.0 + row_mods[:, 3]) + row_mods[:, 4]).astype(float_bf)
    piece = lax.all_gather(h_hidden, "tensor", axis=0, tiled=True)
    rows_hidden = piece
    gate_up = jnp.einsum("rd,tdf->rtf", piece, hidden_weight, preferred_element_type=jnp.float32)
    gate_pre = gate_up[:, 0]
    up_pre = gate_up[:, 1]
    active = (jax.nn.silu(gate_pre) * up_pre).astype(float_bf)
    out_hidden = lax.psum_scatter(
        jnp.dot(active, down_weight, preferred_element_type=jnp.float32).astype(jnp.bfloat16),
        "tensor",
        scatter_dimension=0,
        tiled=True,
    ).astype(jnp.float32)
    gate_hidden = jax.nn.sigmoid(row_mods[:, 5])
    final = middle + row_mask * gate_hidden * out_hidden
    grad_final = cotangent.astype(jnp.float32)
    grad_out_hidden = (grad_final * row_mask * gate_hidden).astype(float_bf)
    grad_gate_hidden = grad_final * row_mask * out_hidden * gate_hidden * (1.0 - gate_hidden)
    piece = lax.all_gather(grad_out_hidden, "tensor", axis=0, tiled=True)
    grad_active = jnp.einsum("rd,fd->rf", piece, down_weight, preferred_element_type=jnp.float32)
    sig_gate = jax.nn.sigmoid(gate_pre)
    grad_gate = grad_active * up_pre * sig_gate * (1.0 + gate_pre * (1.0 - sig_gate))
    grad_up = grad_active * gate_pre * sig_gate
    rows_grad_hidden = piece
    grad_gate_up = jnp.stack([grad_gate, grad_up], axis=1).astype(float_bf)
    grad_down = jnp.einsum(
        "rf,rd->fd", active, rows_grad_hidden, preferred_element_type=jnp.float32
    )
    grad_hidden_w = jnp.einsum(
        "rd,rtf->tdf", rows_hidden, grad_gate_up, preferred_element_type=jnp.float32
    )
    grad_h_hidden = lax.psum_scatter(
        jnp.einsum(
            "rtf,tdf->rd", grad_gate_up, hidden_weight, preferred_element_type=jnp.float32
        ).astype(jnp.bfloat16),
        "tensor",
        scatter_dimension=0,
        tiled=True,
    ).astype(jnp.float32)
    grad_middle = grad_final + norm_back(
        grad_h_hidden * (1.0 + row_mods[:, 3]), norm_hidden, inverse_hidden
    )
    grad_out_attend = (grad_middle * row_mask * gate_attend).astype(float_bf)
    grad_gate_attend = grad_middle * row_mask * out_attend * gate_attend * (1.0 - gate_attend)
    piece = lax.all_gather(grad_out_attend, "tensor", axis=0, tiled=True)
    grad_attended = jnp.einsum(
        "rd,ed->re", piece, output_weight, preferred_element_type=jnp.float32
    ).astype(float_bf)
    grad_output_w = jnp.einsum("re,rd->ed", attended, piece, preferred_element_type=jnp.float32)
    grad_heads = grad_attended.reshape(chain_count, chain_span, heads_local, HD)
    logits_again = scores_of(query_rows, key_rows, bias_full, keep_mask)
    probs_exact = jnp.exp(logits_again - log_total)
    grad_value = jnp.einsum(
        "chqk,cqhd->ckhd",
        probs_exact.astype(float_bf),
        grad_heads,
        preferred_element_type=jnp.float32,
    )
    grad_probs = jnp.einsum(
        "cqhd,ckhd->chqk", grad_heads, value_rows, preferred_element_type=jnp.float32
    )
    grad_logits = (
        probs_exact * (grad_probs - jnp.sum(grad_probs * probs_exact, axis=-1, keepdims=True))
    ).astype(float_bf)
    grad_query = jnp.einsum(
        "chqk,ckhd->cqhd", grad_logits, key_rows, preferred_element_type=jnp.float32
    ) * HD ** (-0.5)
    grad_key = jnp.einsum(
        "chqk,cqhd->ckhd", grad_logits, query_rows, preferred_element_type=jnp.float32
    ) * HD ** (-0.5)
    grad_projected = jnp.stack(
        [
            grad_query.reshape(group_rows, heads_local * HD),
            grad_key.reshape(group_rows, heads_local * HD),
            grad_value.reshape(group_rows, heads_local * HD),
        ],
        axis=1,
    ).astype(float_bf)
    grad_bias_local = lax.all_to_all(grad_logits, "tensor", split_axis=2, concat_axis=1, tiled=True)
    grad_pair = jnp.einsum(
        "chij,ph->cijp", grad_bias_local, bias_weight, preferred_element_type=jnp.float32
    ).astype(float_bf)
    grad_bias_w = jnp.einsum(
        "cijp,chij->ph", pair_features, grad_bias_local, preferred_element_type=jnp.float32
    )
    grad_input_w = jnp.einsum(
        "rd,rte->tde", rows_attend, grad_projected, preferred_element_type=jnp.float32
    )
    grad_h_attend = lax.psum_scatter(
        jnp.einsum(
            "rte,tde->rd", grad_projected, input_weight, preferred_element_type=jnp.float32
        ).astype(jnp.bfloat16),
        "tensor",
        scatter_dimension=0,
        tiled=True,
    ).astype(jnp.float32)
    grad_tokens = grad_middle + norm_back(
        grad_h_attend * (1.0 + row_mods[:, 0]), norm_attend, inverse_attend
    )
    grad_row_mods = jnp.stack(
        [
            grad_h_attend * norm_attend,
            grad_h_attend,
            grad_gate_attend,
            grad_h_hidden * norm_hidden,
            grad_h_hidden,
            grad_gate_hidden,
        ],
        axis=1,
    ).reshape(local_rows, 6 * model_width)
    grad_modulation = jnp.dot(select.T, grad_row_mods, precision=HIGH)
    chain_mods = lax.psum(grad_modulation.astype(jnp.bfloat16), "tensor").astype(jnp.float32)
    all_mods, all_condition, all_time_hot, all_class_hot = (
        lax.all_gather(chain_mods.astype(jnp.bfloat16), "dp", axis=0, tiled=True).astype(
            chain_mods.dtype
        ),
        lax.all_gather(condition.astype(jnp.bfloat16), "dp", axis=0, tiled=True).astype(
            condition.dtype
        ),
        lax.all_gather(time_hot.astype(jnp.bfloat16), "dp", axis=0, tiled=True).astype(
            time_hot.dtype
        ),
        lax.all_gather(class_hot.astype(jnp.bfloat16), "dp", axis=0, tiled=True).astype(
            class_hot.dtype
        ),
    )
    grad_mod_w = jnp.dot(all_condition.T, all_mods, precision=HIGH)
    grad_condition = jnp.dot(all_mods, mod_weight.T, precision=HIGH)
    grad_time = jnp.dot(all_time_hot.T, grad_condition, precision=HIGH)
    grad_class = jnp.dot(all_class_hot.T, grad_condition, precision=HIGH)
    bias_total = lax.psum(grad_bias_w, ("dp", "tensor"))
    shared_sums = (bias_total, grad_mod_w, grad_time, grad_class)
    weight_list = (
        lax.psum_scatter(grad_input_w, "dp", scatter_dimension=1, tiled=True),
        lax.psum_scatter(grad_output_w, "dp", scatter_dimension=1, tiled=True),
        lax.psum_scatter(grad_hidden_w, "dp", scatter_dimension=1, tiled=True),
        lax.psum_scatter(grad_down, "dp", scatter_dimension=1, tiled=True),
    )
    return (
        final.astype(float_bf),
        grad_tokens.astype(float_bf),
        grad_pair,
        shared_sums[0],
        weight_list[0],
        weight_list[1],
        weight_list[2],
        weight_list[3],
        shared_sums[1],
        shared_sums[2],
        shared_sums[3],
    )


def solution(mesh):
    placed = (
        P(("dp", "tensor"), None),
        P("dp", "tensor", None, None),
        P(("dp", "tensor"), None),
        P("dp"),
        P("dp"),
        P("dp"),
        P(),
        P(None, None, "tensor"),
        P("tensor", None),
        P(None, None, "tensor"),
        P("tensor", None),
        P(),
        P(),
        P(),
    )
    return jax.shard_map(
        body,
        mesh=mesh,
        in_specs=placed,
        out_specs=(
            P(("dp", "tensor"), None),
            P(("dp", "tensor"), None),
            P("dp", "tensor", None, None),
            P(),
            P(None, "dp", "tensor"),
            P("tensor", "dp"),
            P(None, "dp", "tensor"),
            P("tensor", "dp"),
            P(),
            P(),
            P(),
        ),
        check_vma=False,
    )
```

profile of v0, /device:TPU:0, one launch (start us, length us, event | category | flops | bytes accessed | tf_op | source)
XLA Modules:
  0.0 592.7 jit_solution(17388391469659766945)
XLA Ops:
  7.2 11.4 %fusion = bf16[2,12,64,256]{3,1,2,0:T(8,128)(2,1)} fusion(bf16[2,64,256,256]{3,2,1,0:T(8,128)(2,1)} %param.15, bf16[256,12]{0,1:T(8,128)(2,1)} %param.20), kind=kOutput, calls=%fused_computation.21 | convolution fusion | flops 201719808 | bytes 17569792 | tf_op jit(solution)/shard_map/cijp,ph->chij/dot_general | solution.py:78
  21.0 4.2 all-to-all-start
  35.4 10.1 %all_gather.24 = bf16[512,768]{1,0:T(8,128)(2,1)S(1)} all-gather(bf16[128,768]{1,0:T(8,128)(2,1)S(1)} %fusion.23), channel_id=1, replica_groups=mesh['dp'=8,'tensor'=4] {'tensor'}, dimensions={0}, use_global_device_ids=true | all-gather | bytes 983040 | tf_op jit(solution)/shard_map/all_gather | solution.py:82
  67.1 22.3 %reduce-scatter.12.cloned.1.call-done = f32[128,768]{1,0:T(8,128)} async-done(((f32[512,768]{1,0:T(8,128)}), f32[128,768]{1,0:T(8,128)}) %reduce-scatter.12.cloned.1.call-update) | async-done | bytes 393232 | tf_op jit(solution)/shard_map/reduce_scatter | solution.py:99
  92.5 8.2 %all_gather.25 = bf16[512,768]{1,0:T(8,128)(2,1)S(1)} all-gather(bf16[128,768]{1,0:T(8,128)(2,1)S(1)} %fusion.43), channel_id=1, replica_groups=mesh['dp'=8,'tensor'=4] {'tensor'}, dimensions={0}, use_global_device_ids=true | all-gather | bytes 983040 | tf_op jit(solution)/shard_map/all_gather | solution.py:109
  100.7 8.9 %all_gather.26 = bf16[512,768]{1,0:T(8,128)(2,1)S(1)} all-gather(bf16[128,768]{1,0:T(8,128)(2,1)S(1)} %get-tuple-element.87), channel_id=1, replica_groups=mesh['dp'=8,'tensor'=4] {'tensor'}, dimensions={0}, use_global_device_ids=true | all-gather | bytes 983040 | tf_op jit(solution)/shard_map/all_gather | solution.py:126
  120.2 20.4 %reduce-scatter.16.cloned.1.call-done = bf16[128,768]{1,0:T(8,128)(2,1)} async-done(((bf16[512,768]{1,0:T(8,128)(2,1)}), bf16[128,768]{1,0:T(8,128)(2,1)}) %reduce-scatter.16.cloned.1.call-update) | async-done | bytes 196624 | tf_op jit(solution)/shard_map/reduce_scatter | solution.py:139
  141.8 24.7 %reduce-scatter.14.cloned.1.call-done = bf16[128,768]{1,0:T(8,128)(2,1)} async-done(((bf16[512,768]{1,0:T(8,128)(2,1)}), bf16[128,768]{1,0:T(8,128)(2,1)}) %reduce-scatter.14.cloned.1.call-update) | async-done | bytes 196624 | tf_op jit(solution)/shard_map/reduce_scatter | solution.py:115
  168.8 8.3 %all_gather.27 = bf16[512,768]{1,0:T(8,128)(2,1)S(1)} all-gather(bf16[128,768]{1,0:T(8,128)(2,1)S(1)} %get-tuple-element.70), channel_id=1, replica_groups=mesh['dp'=8,'tensor'=4] {'tensor'}, dimensions={0}, use_global_device_ids=true | all-gather | bytes 983040 | tf_op jit(solution)/shard_map/all_gather | solution.py:152
  189.1 5.0 convolution_bitcast_fusion
  194.1 8.2 %copy.189 = f32[2,768,768]{2,0,1:T(2,128)} copy(f32[2,768,768]{1,2,0:T(8,128)} %convolution_bitcast_fusion) | data formatting | bytes 9437184 | tf_op jit(solution)/shard_map/rd,rtf->tdf/transpose | solution.py:136
  205.2 4.2 copy.201
  209.5 4.7 reshape.182
  220.3 20.5 %all-gather = bf16[8,2,256]{2,1,0:T(2,128)(2,1)S(1)} all-gather(bf16[1,2,256]{2,1,0:T(2,128)(2,1)S(1)} %convert_bitcast_fusion.3), channel_id=1, replica_groups=mesh['dp'=8,'tensor'=4] {'dp'}, dimensions={0}, use_global_device_ids=true | all-gather | bytes 9216 | tf_op jit(solution)/shard_map/all_gather | solution.py:224
  242.1 16.2 %all-gather.3 = bf16[8,2,64]{2,1,0:T(2,128)(2,1)S(1)} all-gather(bf16[1,2,64]{2,1,0:T(2,128)(2,1)S(1)} %fusion.66), channel_id=1, replica_groups=mesh['dp'=8,'tensor'=4] {'dp'}, dimensions={0}, use_global_device_ids=true | all-gather | bytes 2304 | tf_op jit(solution)/shard_map/all_gather | solution.py:230
  258.3 18.2 %all-gather.2 = bf16[8,2,64]{2,1,0:T(2,128)(2,1)S(1)} all-gather(bf16[1,2,64]{2,1,0:T(2,128)(2,1)S(1)} %fusion.65), channel_id=1, replica_groups=mesh['dp'=8,'tensor'=4] {'dp'}, dimensions={0}, use_global_device_ids=true | all-gather | bytes 2304 | tf_op jit(solution)/shard_map/all_gather | solution.py:227
  278.9 8.2 %convolution_bitcast_fusion.3 = f32[256,12]{0,1:T(8,128)S(1)} fusion(bf16[2,64,256,256]{3,2,1,0:T(8,128)(2,1)} %param.15, bf16[2,12,64,256]{3,2,1,0:T(8,128)(2,1)S(1)} %bitcast.226), kind=kOutput, calls=%fused_computation.35 | convolution fusion | flops 201326592 | bytes 17575936 | tf_op jit(solution)/shard_map/cijp,chij->ph/dot_general | solution.py:190
  287.1 43.0 %psum.14 = f32[256,12]{0,1:T(8,128)} all-reduce(f32[256,12]{0,1:T(8,128)S(1)} %convolution_bitcast_fusion.3), channel_id=1, replica_groups=mesh['dp'=8,'tensor'=4] {'dp','tensor'}, use_global_device_ids=true, to_apply=%region_16.17 | all-reduce | flops 3072 | bytes 24576 | tf_op jit(solution)/shard_map/psum | solution.py:238
  330.1 8.6 %convolution_convert_fusion = bf16[2,64,256,256]{3,2,1,0:T(8,128)(2,1)} fusion(bf16[2,12,64,256]{3,2,1,0:T(8,128)(2,1)S(1)} %bitcast.227, bf16[256,12]{0,1:T(8,128)(2,1)S(1)} %copy-done.39), kind=kOutput, calls=%fused_computation | convolution fusion | flops 209715200 | bytes 17569792 | tf_op jit(solution)/shard_map/chij,ph->cijp/dot_general | solution.py:187
  353.6 11.6 %psum.15 = bf16[2,4608]{1,0:T(2,128)(2,1)S(1)} all-reduce(bf16[2,4608]{1,0:T(2,128)(2,1)S(1)} %convolution_convert_fusion.1), channel_id=1, replica_groups=mesh['dp'=8,'tensor'=4] {'tensor'}, use_global_device_ids=true, to_apply=%region_21.22 | all-reduce | flops 9216 | bytes 36864 | tf_op jit(solution)/shard_map/psum | solution.py:219
  365.2 31.0 %all-gather.1 = bf16[8,2,4608]{2,1,0:T(2,128)(2,1)S(1)} all-gather(bf16[1,2,4608]{2,1,0:T(2,128)(2,1)S(1)} %bitcast.241), channel_id=1, replica_groups=mesh['dp'=8,'tensor'=4] {'dp'}, dimensions={0}, use_global_device_ids=true | all-gather | bytes 165888 | tf_op jit(solution)/shard_map/all_gather | solution.py:221
  402.8 41.2 %all-reduce.3.cloned.1.call-done = f32[2,768,768]{2,0,1:T(2,128)} async-done(((f32[2,768,768]{2,0,1:T(2,128)}), f32[2,768,768]{2,0,1:T(2,128)}) %all-reduce.3.cloned.1.call-update) | async-done | bytes 4718608
  446.0 67.9 %reduce-scatter.22.cloned.1.call-done = f32[96,576]{1,0:T(8,128)} async-done(((f32[768,576]{1,0:T(8,128)}), f32[96,576]{1,0:T(8,128)}) %reduce-scatter.22.cloned.1.call-update) | async-done | bytes 221200
  515.7 70.1 %reduce-scatter.20.cloned.1.call-done = f32[768,96]{0,1:T(8,128)} async-done(((f32[768,768]{0,1:T(8,128)}), f32[768,96]{0,1:T(8,128)}) %reduce-scatter.20.cloned.1.call-update) | async-done | bytes 294928 | tf_op jit(solution)/shard_map/reduce_scatter | solution.py:244
  (243 shorter events, 100.2 us)
Async XLA Ops:
  7.2 102.4 %copy-start = (bf16[2,768,768]{2,1,0:T(8,128)(2,1)S(1)}, bf16[2,768,768]{2,1,0:T(8,128)(2,1)}, u32[]{:S(2)}) copy-start(bf16[2,768,768]{2,1,0:T(8,128)(2,1)} %param.23) | copy-start | bytes 7077892
  21.0 27.3 %all-to-all-start = ((bf16[2,12,64,256]{3,2,0,1:T(8,128)(2,1)}), bf16[2,12,64,256]{3,2,0,1:T(8,128)(2,1)}, u32[]{:S(2)}, u32[]{:S(2)}) async-start(bf16[2,12,64,256]{3,2,0,1:T(8,128)(2,1)} %copy.162), calls=%async_computation | async-start | bytes 1572864 | tf_op jit(solution)/shard_map/all_to_all | solution.py:81
  25.2 64.2 %reduce-scatter.12.cloned.1.call-start = ((), (), s32[]{:S(2)}) async-start(), calls=%async_computation.9 | async-start | bytes 1966080 | tf_op jit(solution)/shard_map/reduce_scatter | solution.py:99
  25.3 41.1 %copy-start.50 = (s32[128]{0:T(128)}, s32[128]{0:T(128)S(1)}, u32[]{:S(2)}) copy-start(s32[128]{0:T(128)S(1)} %and_select_fusion) | copy-start | bytes 1540
  59.5 81.1 %reduce-scatter.16.cloned.1.call-start = ((), (), s32[]{:S(2)}) async-start(), calls=%async_computation.11 | async-start | bytes 983040 | tf_op jit(solution)/shard_map/reduce_scatter | solution.py:139
  116.9 49.7 %reduce-scatter.14.cloned.1.call-start = ((), (), s32[]{:S(2)}) async-start(), calls=%async_computation.10 | async-start | bytes 983040 | tf_op jit(solution)/shard_map/reduce_scatter | solution.py:115
  120.1 46.4 %copy-start.9 = (f32[128,1,768]{2,0,1:T(8,128)S(1)}, f32[128,1,768]{2,0,1:T(8,128)}, u32[]{:S(2)}) copy-start(f32[128,1,768]{2,0,1:T(8,128)} %copy.209) | copy-start | bytes 1179652
  120.1 46.4 %copy-start.11 = (f32[128,1,768]{2,0,1:T(8,128)S(1)}, f32[128,1,768]{2,0,1:T(8,128)}, u32[]{:S(2)}) copy-start(f32[128,1,768]{2,0,1:T(8,128)} %copy.206) | copy-start | bytes 1179652
  120.1 46.4 %copy-start.28 = (bf16[128,768]{1,0:T(8,128)(2,1)S(1)}, bf16[128,768]{1,0:T(8,128)(2,1)}, u32[]{:S(2)}) copy-start(bf16[128,768]{1,0:T(8,128)(2,1)} %param.16) | copy-start | bytes 589828
  120.1 46.4 %copy-start.48 = (f32[128]{0:T(128)S(1)}, f32[128]{0:T(128)}, u32[]{:S(2)}) copy-start(f32[128]{0:T(128)} %copy-done.47) | copy-start | bytes 1540
  120.2 218.6 %reduce-scatter.24.cloned.1.call-start = ((), (), s32[]{:S(2)}) async-start(), calls=%async_computation.15 | async-start | bytes 884736
  180.6 159.9 %reduce-scatter.18.cloned.1.call-start = ((), (), s32[]{:S(2)}) async-start(), calls=%async_computation.12 | async-start | bytes 983040 | tf_op jit(solution)/shard_map/reduce_scatter | solution.py:196
  189.0 255.0 %all-reduce.3.cloned.1.call-start = ((), (), s32[]{:S(2)}) async-start(), calls=%async_computation.16 | async-start | bytes 9437184
  202.3 311.5 %reduce-scatter.22.cloned.1.call-start = ((), (), s32[]{:S(2)}) async-start(), calls=%async_computation.14 | async-start | bytes 2211840
  214.8 26.0 %copy-start.60 = (u32[32]{0:T(128)S(1)}, u32[32]{0:T(128)}, u32[]{:S(2)}) copy-start(u32[32]{0:T(128)} %constant.68) | copy-start | bytes 388
  214.8 43.4 %copy-start.59 = (s32[2]{0:T(128)S(1)}, s32[2]{0:T(128)}, u32[]{:S(2)}) copy-start(s32[2]{0:T(128)} %param.18) | copy-start | bytes 28
  214.9 61.6 %copy-start.20 = (bf16[512,768]{1,0:T(8,128)(2,1)S(1)}, bf16[512,768]{1,0:T(8,128)(2,1)}, u32[]{:S(2)}) copy-start(bf16[512,768]{1,0:T(8,128)(2,1)} %copy-done.19) | copy-start | bytes 2359300
  214.9 61.6 %copy-start.21 = (bf16[512,768]{1,0:T(8,128)(2,1)S(1)}, bf16[512,768]{1,0:T(8,128)(2,1)}, u32[]{:S(2)}) copy-start(bf16[512,768]{1,0:T(8,128)(2,1)} %get-tuple-element.76) | copy-start | bytes 2359300
  216.7 62.1 %all-to-all-start.1 = ((bf16[2,3,256,256]{3,0,1,2:T(2,128)(2,1)}), bf16[2,3,256,256]{3,0,1,2:T(2,128)(2,1)S(1)}, u32[]{:S(2)}, u32[]{:S(2)}) async-start(bf16[2,3,256,256]{3,0,1,2:T(2,128)(2,1)} %copy.183), calls=%async_computation.5 | async-start | bytes 1572864 | tf_op jit(solution)/shard_map/all_to_all | solution.py:186
  220.2 365.7 %reduce-scatter.20.cloned.1.call-start = ((), (), s32[]{:S(2)}) async-start(), calls=%async_computation.13 | async-start | bytes 2654208 | tf_op jit(solution)/shard_map/reduce_scatter | solution.py:244
  278.9 51.2 %copy-start.39 = (bf16[256,12]{0,1:T(8,128)(2,1)S(1)}, bf16[256,12]{0,1:T(8,128)(2,1)}, u32[]{:S(2)}) copy-start(bf16[256,12]{0,1:T(8,128)(2,1)} %param.20) | copy-start | bytes 18436
  350.7 45.6 %copy-start.18 = (bf16[128,768]{1,0:T(8,128)(2,1)S(1)}, bf16[128,768]{1,0:T(8,128)(2,1)}, u32[]{:S(2)}) copy-start(bf16[128,768]{1,0:T(8,128)(2,1)} %reduce-scatter.18.cloned.1.call-done) | copy-start | bytes 589828
  350.7 45.9 %copy-start.5 = (bf16[256,4608]{1,0:T(8,128)(2,1)S(1)}, bf16[256,4608]{1,0:T(8,128)(2,1)}, u32[]{:S(2)}) copy-start(bf16[256,4608]{1,0:T(8,128)(2,1)} %param.25) | copy-start | bytes 7077892
  399.9 186.0 %copy-start.1 = (bf16[2,768,768]{2,1,0:T(8,128)(2,1)S(1)}, bf16[2,768,768]{2,1,0:T(8,128)(2,1)}, u32[]{:S(2)}) copy-start(bf16[2,768,768]{2,1,0:T(8,128)(2,1)} %param.23) | copy-start | bytes 7077892
  (47 other events, 276.3 us)
Sparse Core Ops, SparseCore 0:
  59.7 29.7 reduce-scatter.11
  117.0 23.6 reduce-scatter.15
  143.2 23.2 reduce-scatter.13
  180.7 62.8 reduce-scatter.23
  245.9 22.2 reduce-scatter.17
  272.2 171.8 all-reduce.2
  447.9 65.9 reduce-scatter.21
  517.9 67.8 reduce-scatter.19
where the time goes:
time: 594 us; the launch traced here: 593 us
  waiting for transfers between devices  247 us (42%)
  blocking collectives  176 us (30%)
  matrix products  72.9 us (12%)
  local copies, waits for them, and re-layouts  55.4 us (9%)
  other arithmetic  17.9 us (3%)
  between operations  15.5 us (3%)
  starting transfers between devices  8.25 us (1%)
    unnamed x11, waiting for transfers between devices  109 us
    reduce_scatter x1, waiting for transfers between devices, body(): lax.psum_scatter(grad_down, 'dp', scatter_dimension=1, tiled=True)  70.1 us
    psum x1, blocking collectives, body(): bias_total = lax.psum(grad_bias_w, ('dp', 'tensor'))  43 us
    all_gather x1, blocking collectives, body(): lax.all_gather(chain_mods.astype(jnp.bfloat16), 'dp', axis=0, tiled=True)  31 us
    unnamed x141, local copies, waits for them, and re-layouts  28.9 us
    reduce_scatter x1, waiting for transfers between devices, body(): lax.psum_scatter(jnp.dot(active, down_weight, preferred_element_type=jnp....  24.7 us
    reduce_scatter x1, waiting for transfers between devices, body(): lax.psum_scatter(jnp.dot(attended, output_weight, preferred_element_type=...  22.3 us
    all_gather x1, blocking collectives, body(): lax.all_gather(condition.astype(jnp.bfloat16), 'dp', axis=0, tiled=True)  20.5 us
  transfers between devices with their start and end apart: 10, of which 6 were waited for; matrix products, arithmetic and copies ran while one was open for 17% of the time, Pallas kernels for 0%

commit v1 on v0

v1 whole, which is shorter than its diff:
```python
import functools

import jax
import jax.numpy as jnp
from jax import lax
from jax.experimental import pallas as pl
from jax.experimental.pallas import tpu as pltpu
from jax.sharding import PartitionSpec as P

HD = 64
EPSILON = 1e-05
BF = jnp.bfloat16
F32 = jnp.float32
MESH = pl.DeviceIdType.MESH
PAIR_SLOTS = 4
PAIR_ROWS = 16
VMEM_BYTES = 60 << 20


def nn(a, b):
    return lax.dot_general(a, b, (((1,), (0,)), ((), ())), preferred_element_type=F32)


def nt(a, b):
    return lax.dot_general(a, b, (((1,), (1,)), ((), ())), preferred_element_type=F32)


def tn(a, b):
    return lax.dot_general(a, b, (((0,), (0,)), ((), ())), preferred_element_type=F32)


def sigmoid(x):
    return 1.0 / (1.0 + jnp.exp(-x))


def layer_norm(rows):
    centre = rows - jnp.mean(rows, axis=-1, keepdims=True)
    inverse = lax.rsqrt(jnp.mean(centre * centre, axis=-1, keepdims=True) + EPSILON)
    return centre * inverse, inverse


def norm_back(grad, normed, inverse):
    return inverse * (
        grad
        - jnp.mean(grad, axis=-1, keepdims=True)
        - normed * jnp.mean(grad * normed, axis=-1, keepdims=True)
    )


class Remote:
    def __init__(self, send_sems, recv_sems):
        self.send_sems, self.recv_sems, self.started = send_sems, recv_sems, []

    def start(self, src, dst, device):
        index = len(self.started)
        copy = pltpu.make_async_remote_copy(
            src_ref=src,
            dst_ref=dst,
            send_sem=self.send_sems.at[index],
            recv_sem=self.recv_sems.at[index],
            device_id=device,
            device_id_type=MESH,
        )
        copy.start()
        self.started.append(copy)
        return copy

    def finish(self):
        for copy in self.started:
            copy.wait_send()


class Gather:
    def __init__(self, remote, slots, here, near, far, near_device, far_device):
        self.remote, self.slots, self.far, self.near_device = remote, slots, far, near_device
        self.to_far = remote.start(slots.at[here], slots.at[here], far_device)
        self.to_near = remote.start(slots.at[here], slots.at[here], near_device)

    def forward(self):
        self.to_far.wait_recv()
        self.passed = self.remote.start(
            self.slots.at[self.far], self.slots.at[self.far], self.near_device
        )

    def wait_near(self):
        self.to_near.wait_recv()

    def wait_rest(self):
        self.passed.wait_recv()


class Scatter:
    def __init__(self, remote, part, out, arrived, ids, near_device, far_device):
        self.remote, self.part, self.out, self.arrived = remote, part, out, arrived
        self.here, self.near, self.far, self.cross = ids
        self.near_device, self.far_device = near_device, far_device

    def pre(self):
        self.out[0] = self.part[self.cross].astype(BF)
        self.first = self.remote.start(self.out.at[0], self.arrived.at[0], self.near_device)

    def across(self):
        self.first.wait_recv()
        self.out[1] = (self.part[self.far] + self.arrived[0].astype(F32)).astype(BF)
        self.second = self.remote.start(self.out.at[1], self.arrived.at[1], self.far_device)

    def local(self):
        self.out[2] = self.part[self.near].astype(BF)
        self.third = self.remote.start(self.out.at[2], self.arrived.at[2], self.near_device)
        self.own = self.part[self.here]

    def total(self):
        self.third.wait_recv()
        self.second.wait_recv()
        return self.own + self.arrived[2].astype(F32) + self.arrived[1].astype(F32)


class Halving:
    def __init__(self, remote, store, arrived, rank, count, device, order):
        self.remote, self.store, self.arrived = remote, store, arrived
        self.rank, self.count, self.device = rank, count, device
        self.order, self.step, self.offset, self.landing = order, 0, 0, 0

    def send(self):
        bit = self.order[self.step]
        self.half = self.count >> (self.step + 1)
        mine = lax.rem(self.rank // (1 << bit), 2)
        partner = self.rank + (1 - 2 * mine) * (1 << bit)
        away = self.offset + (1 - mine) * self.half
        self.offset = self.offset + mine * self.half
        self.copy = self.remote.start(
            self.store.at[pl.ds(away, self.half)],
            self.arrived.at[pl.ds(self.landing, self.half)],
            self.device(partner),
        )

    def sum(self):
        self.copy.wait_recv()
        keep = pl.ds(self.offset, self.half)
        total = self.store[keep].astype(F32) + self.arrived[
            pl.ds(self.landing, self.half)
        ].astype(F32)
        self.landing += self.half
        self.step += 1
        if self.step == len(self.order):
            return total[0]
        self.store[keep] = total.astype(BF)
        self.send()
        return None

    def last(self):
        total = None
        while total is None:
            total = self.sum()
        return total


def slot_of(chunk, order):
    slot = 0
    for bit in order:
        slot = slot * 2 + (chunk >> bit) % 2
    return slot


def layer_kernel(
    dims,
    orders,
    length_ref,
    time_ref,
    class_ref,
    tokens_hbm,
    cotangent_hbm,
    pair_hbm,
    bias_hbm,
    input_hbm,
    output_hbm,
    hidden_hbm,
    down_hbm,
    modulation_hbm,
    time_hbm,
    class_hbm,
    result_out,
    grad_tokens_out,
    scores_out,
    mods_out,
    hots_out,
    bias_grad_out,
    weights_out,
    tokens,
    cotangent,
    pair,
    bias_weight,
    input_weight,
    output_weight,
    hidden_weight,
    down_weight,
    modulation_weight,
    tables,
    mods,
    stage,
    hots,
    mods_all,
    rows_attend,
    rows_hidden,
    rows_down,
    rows_out,
    bias_send,
    bias_full,
    queries,
    keys,
    values,
    probs,
    attended,
    part,
    part_down,
    grad_active,
    active,
    grad_gate,
    grad_up,
    grad_scores,
    scores_own,
    grad_projected,
    scatter_send,
    scatter_recv,
    turned,
    turned_more,
    grad_store,
    grad_recv,
    final_weights,
    norm_attend,
    norm_hidden,
    middle,
    out_attend,
    grad_middle,
    result,
    grad_tokens,
    mod_part,
    mod_near,
    mod_sum,
    mod_far,
    bias_grads,
    bias_sums,
    bias_grad,
    load_sems,
    pair_sems,
    store_sems,
    send_sems,
    recv_sems,
):
    (groups, chains, span, local, width, local_width, queries_local, hidden) = dims
    heads = local_width // HD
    dp = lax.axis_index("dp")
    me = lax.axis_index("tensor")
    core = lax.rem(me, 2)
    chip = me // 2
    near = me + 1 - 2 * core
    far = lax.rem(me + 2, 4)
    cross = 3 - me
    away = 1 - chip
    near_device, far_device, cross_device = (dp, near), (dp, far), (dp, cross)

    def dp_device(index):
        return (index, me)

    barrier = pltpu.get_barrier_semaphore()
    for device in (near_device, far_device, cross_device):
        pl.semaphore_signal(barrier, inc=1, device_id=device, device_id_type=MESH)
    for step in range(1, groups):
        pl.semaphore_signal(
            barrier, inc=1, device_id=dp_device(lax.rem(dp + step, groups)), device_id_type=MESH
        )

    loads = []

    def load(src, dst):
        copy = pltpu.make_async_copy(src, dst, load_sems.at[len(loads)])
        copy.start()
        loads.append(copy)
        return copy

    blocks = queries_local // PAIR_ROWS
    n_blocks = chains * blocks

    def pair_copy(index):
        chain = lax.rem(chip + index // blocks, chains)
        slot = lax.rem(index, PAIR_SLOTS)
        return pltpu.make_async_copy(
            pair_hbm.at[chain, pl.ds(lax.rem(index, blocks) * PAIR_ROWS, PAIR_ROWS)],
            pair.at[slot],
            pair_sems.at[slot],
        )

    times = time_hbm.shape[0]
    load_time = load(time_hbm, tables.at[pl.ds(0, times)])
    load_class = load(class_hbm, tables.at[pl.ds(times, class_hbm.shape[0])])
    load_tokens = load(tokens_hbm, tokens)
    load_modulation = load(modulation_hbm, modulation_weight)
    load_cotangent = load(cotangent_hbm, cotangent)
    load_bias = load(bias_hbm, bias_weight)
    for index in range(PAIR_SLOTS):
        pair_copy(index).start()
    load_input = load(input_hbm, input_weight)
    load_output = load(output_hbm, output_weight)
    load_down = load(down_hbm, down_weight)
    load_hidden = load(hidden_hbm, hidden_weight)

    remote = Remote(send_sems, recv_sems)

    n_table = tables.shape[0]
    lane = lax.broadcasted_iota(jnp.int32, (16, n_table), 1)
    row = lax.broadcasted_iota(jnp.int32, (16, n_table), 0)
    picked = ((row == 0) & (lane == time_ref[chip])) | (
        (row == 1) & (lane == times + class_ref[chip])
    )
    time_row = jnp.where(row < 8, time_ref[0], time_ref[1])
    class_row = jnp.where(row < 8, class_ref[0], class_ref[1])
    hots[dp] = jnp.where((lane == time_row) | (lane == times + class_row), 1.0, 0.0).astype(BF)
    load_time.wait()
    load_class.wait()
    condition = nn(jnp.where(picked, 1.0, 0.0).astype(BF), tables[...]).astype(BF)
    load_modulation.wait()
    both = nn(condition, modulation_weight[...])
    mods[...] = jnp.broadcast_to(both[0:1] + both[1:2], mods.shape)

    def mod(index):
        return mods[0:1, index * width : (index + 1) * width]

    place = lax.rem(me * local, span) + lax.broadcasted_iota(jnp.int32, (local, 1), 0)
    valid = jnp.where(place < length_ref[chip], 1.0, 0.0)

    load_tokens.wait()
    normed, inverse_attend = layer_norm(tokens[...].astype(F32))
    norm_attend[...] = normed
    rows_attend[me] = (normed * (1.0 + mod(0)) + mod(1)).astype(BF)
    load_cotangent.wait()
    gate_hidden = sigmoid(mod(5))
    rows_down[me] = (cotangent[...].astype(F32) * valid * gate_hidden).astype(BF)
    load_bias.wait()
    wide = jnp.concatenate(
        [
            bias_weight[...].astype(F32),
            jnp.zeros((bias_weight.shape[0], 128 - bias_weight.shape[1]), F32),
        ],
        axis=1,
    )
    bias_turned = jnp.transpose(wide)[:16].astype(BF)

    pl.semaphore_wait(barrier, 3 + groups - 1)
    gather_attend = Gather(remote, rows_attend, me, near, far, near_device, far_device)
    hot_copies = []
    for step in range(1, groups):
        device = dp_device(lax.rem(dp + step, groups))
        hot_copies.append(remote.start(hots.at[dp], hots.at[dp], device))

    def bias_block(index, carry):
        slot = lax.rem(index, PAIR_SLOTS)
        pair_copy(index).wait()
        for row_index in range(PAIR_ROWS):
            product = nt(bias_turned, pair[slot, row_index])
            place_row = lax.rem(index, blocks) * PAIR_ROWS + row_index
            for half in range(2):
                stage[half, pl.ds(place_row, 16, stride=queries_local), :] = product[
                    :, half * 128 : (half + 1) * 128
                ]

        @pl.when(index + PAIR_SLOTS < n_blocks)
        def _():
            pair_copy(index + PAIR_SLOTS).start()

        return carry

    all_rows = 4 * heads * queries_local
    bias_copies = []
    for turn in range(2):
        chain = lax.rem(chip + turn, 2)
        lax.fori_loop(turn * blocks, (turn + 1) * blocks, bias_block, 0)
        for half in range(2):
            bias_send[chain, :, :, half * 128 : (half + 1) * 128] = (
                stage[half, 0:all_rows, :].astype(BF).reshape(4 * heads, queries_local, 128)
            )
        mine = pl.ds(me * queries_local, queries_local)
        sent = []
        for owner, device in ((far, far_device), (cross, cross_device), (near, near_device)):
            sent.append(
                remote.start(
                    bias_send.at[chain, pl.ds(owner * heads, heads)],
                    bias_full.at[chain, :, mine],
                    device,
                )
            )
        bias_copies.append(sent)
        bias_full[chain, :, mine, :] = bias_send[chain, pl.ds(me * heads, heads)]
        if turn == 0:
            gather_attend.forward()

    for index in range(PAIR_SLOTS):
        pair_copy(index).start()

    load_input.wait()

    def project(half):
        rows = rows_attend[pl.ds(2 * half, 2)].reshape(span, width)
        queries[half] = nn(rows, input_weight[0]).astype(BF)
        keys[half] = nn(rows, input_weight[1]).astype(BF)
        values[half] = nn(rows, input_weight[2]).astype(BF)

    gather_attend.wait_near()
    project(chip)
    gather_attend.wait_rest()
    project(away)

    head_lane = lax.broadcasted_iota(jnp.int32, (span, local_width), 1)

    def stacked(rows):
        zero = jnp.zeros_like(rows)
        return jnp.concatenate(
            [
                jnp.where((head_lane >= head * HD) & (head_lane < (head + 1) * HD), rows, zero)
                for head in range(heads)
            ],
            axis=0,
        )

    def choose(pieces):
        out = pieces[-1]
        for head in range(heads - 2, -1, -1):
            out = jnp.where(head_lane < (head + 1) * HD, pieces[head], out)
        return out

    def attend(chain):
        scores = nt(stacked(queries[chain]), keys[chain]) * HD ** (-0.5) + bias_full[
            chain
        ].reshape(heads * span, span).astype(F32)
        key_place = lax.broadcasted_iota(jnp.int32, (heads * span, span), 1)
        scores = jnp.where(key_place < length_ref[chain], scores, -1000000000.0)
        top = jnp.max(scores, axis=-1, keepdims=True)
        weights = jnp.exp(scores - top)
        weights = weights * (1.0 / jnp.sum(weights, axis=-1, keepdims=True))
        probs[chain] = weights
        soft = weights.astype(BF)
        attended[chain] = choose(
            [nn(soft[head * span : (head + 1) * span], values[chain]) for head in range(heads)]
        ).astype(BF)

    def put(target, half, rows):
        target[pl.ds(2 * half, 2)] = rows.reshape(2, local, width)

    ids = (me, near, far, cross)

    def scatter(index, source):
        return Scatter(
            remote,
            source,
            scatter_send.at[index],
            scatter_recv.at[index],
            ids,
            near_device,
            far_device,
        )

    bias_copies[0][0].wait_recv()
    bias_copies[0][1].wait_recv()
    bias_copies[1][2].wait_recv()
    attend(away)
    load_output.wait()
    put(part, away, nn(attended[away], output_weight[...]))
    scatter_attend = scatter(0, part)
    scatter_attend.pre()
    bias_copies[1][0].wait_recv()
    bias_copies[1][1].wait_recv()
    bias_copies[0][2].wait_recv()
    scatter_attend.across()
    gather_down = Gather(remote, rows_down, me, near, far, near_device, far_device)
    attend(chip)
    put(part, chip, nn(attended[chip], output_weight[...]))
    scatter_attend.local()

    load_down.wait()

    def back_down(half):
        rows = rows_down[pl.ds(2 * half, 2)].reshape(span, width)
        grad_active[half] = nt(rows, down_weight[...])
        for slot in range(2):
            place_slot = 2 * half + slot
            turned[:, pl.ds(pl.multiple_of(place_slot * local, local), local)] = jnp.transpose(
                rows[slot * local : (slot + 1) * local]
            )

    gather_down.wait_near()
    back_down(chip)
    gather_down.forward()

    gate_attend = sigmoid(mod(2))
    out_total = scatter_attend.total()
    out_attend[...] = out_total
    total = tokens[...].astype(F32) + valid * gate_attend * out_total
    middle[...] = total
    normed, inverse_hidden = layer_norm(total)
    norm_hidden[...] = normed
    rows_hidden[me] = (normed * (1.0 + mod(3)) + mod(4)).astype(BF)
    gather_hidden = Gather(remote, rows_hidden, me, near, far, near_device, far_device)
    gather_down.wait_rest()
    back_down(away)

    load_hidden.wait()

    def transition(half):
        rows = rows_hidden[pl.ds(2 * half, 2)].reshape(span, width)
        gate = nn(rows, hidden_weight[0])
        up = nn(rows, hidden_weight[1])
        squashed = sigmoid(gate)
        silu = gate * squashed
        active[half] = (silu * up).astype(BF)
        back = grad_active[half]
        grad_gate[half] = (back * up * squashed * (1.0 + gate * (1.0 - squashed))).astype(BF)
        grad_up[half] = (back * silu).astype(BF)

    def back_hidden(half):
        put(
            part,
            half,
            nt(grad_gate[half], hidden_weight[0]) + nt(grad_up[half], hidden_weight[1]),
        )

    gather_hidden.wait_near()
    transition(chip)
    gather_hidden.forward()
    back_hidden(chip)
    put(part_down, chip, nn(active[chip], down_weight[...]))
    gather_hidden.wait_rest()
    transition(away)
    back_hidden(away)
    scatter_hidden = scatter(1, part)
    scatter_hidden.pre()
    put(part_down, away, nn(active[away], down_weight[...]))
    scatter_hidden.across()
    scatter_hidden.local()
    scatter_down = scatter(2, part_down)
    scatter_down.pre()

    chunk = width // groups
    per_block = max(1, 192 // chunk)

    def halving(index):
        return Halving(
            remote,
            grad_store.at[index],
            grad_recv.at[index],
            dp,
            groups,
            dp_device,
            orders[index],
        )

    def weight_grad(index, *pairs):
        for block in range(groups // per_block):
            rows = slice(block * per_block * chunk, (block + 1) * per_block * chunk)
            product = jnp.concatenate([nn(left[rows, :], right) for left, right in pairs], axis=1)
            for inner in range(per_block):
                grad_store[index, slot_of(block * per_block + inner, orders[index])] = product[
                    inner * chunk : (inner + 1) * chunk
                ].astype(BF)

    def flat(ref):
        return ref[...].reshape(chains * span, ref.shape[-1])

    def turn_rows(source, target):
        for slot in range(4):
            target[:, slot * local : (slot + 1) * local] = jnp.transpose(source[slot])

    weight_grad(0, (turned, flat(active)))
    sum_down = halving(0)
    sum_down.send()
    scatter_down.across()
    scatter_down.local()
    turn_rows(rows_hidden, turned_more)
    weight_grad(1, (turned_more, flat(grad_gate)))
    sum_gate = halving(1)
    sum_gate.send()
    weight_grad(2, (turned_more, flat(grad_up)))
    sum_up = halving(2)
    sum_up.send()

    grad_h = scatter_hidden.total()
    normed = norm_hidden[...]
    back = cotangent[...].astype(F32) + norm_back(grad_h * (1.0 + mod(3)), normed, inverse_hidden)
    grad_middle[...] = back
    rows_out[me] = (back * valid * gate_attend).astype(BF)
    gather_out = Gather(remote, rows_out, me, near, far, near_device, far_device)

    def keep_mod(index, rows):
        mod_part[index : index + 1, :] = jnp.sum(rows, axis=0, keepdims=True)

    mod_part[...] = jnp.zeros_like(mod_part)
    keep_mod(3, grad_h * normed)
    keep_mod(4, grad_h)
    keep_mod(2, back * valid * out_attend[...] * gate_attend * (1.0 - gate_attend))
    out_total = scatter_down.total()
    result[...] = (middle[...] + valid * gate_hidden * out_total).astype(BF)
    keep_mod(
        5, cotangent[...].astype(F32) * valid * out_total * gate_hidden * (1.0 - gate_hidden)
    )
    turn_rows(rows_attend, turned)

    score_copies = []

    def back_attend(chain):
        rows = rows_out[pl.ds(2 * chain, 2)].reshape(span, width)
        grad_heads = stacked(nt(rows, output_weight[...]).astype(BF))
        weights = probs[chain]
        grad_probs = nt(grad_heads, values[chain])
        grad_logits = (
            weights * (grad_probs - jnp.sum(grad_probs * weights, axis=-1, keepdims=True))
        ).astype(BF)
        grad_scores[chain] = grad_logits.reshape(heads, span, span)
        sent = []
        for owner, device in ((far, far_device), (cross, cross_device), (near, near_device)):
            sent.append(
                remote.start(
                    grad_scores.at[chain, :, pl.ds(owner * queries_local, queries_local)],
                    scores_own.at[chain, pl.ds(me * heads, heads)],
                    device,
                )
            )
        score_copies.append(sent)
        scores_own[chain, pl.ds(me * heads, heads)] = grad_scores[
            chain, :, pl.ds(me * queries_local, queries_local), :
        ]
        query_stack = stacked(queries[chain])
        grad_query = (
            choose(
                [
                    nn(grad_logits[head * span : (head + 1) * span], keys[chain])
                    for head in range(heads)
                ]
            )
            * HD ** (-0.5)
        ).astype(BF)
        grad_key = (tn(grad_logits, query_stack) * HD ** (-0.5)).astype(BF)
        grad_value = tn(weights.astype(BF), grad_heads).astype(BF)
        grad_projected[chain] = jnp.concatenate([grad_query, grad_key, grad_value], axis=1)
        put(
            part,
            chain,
            nt(grad_query, input_weight[0])
            + nt(grad_key, input_weight[1])
            + nt(grad_value, input_weight[2]),
        )

    gather_out.wait_near()
    gather_out.forward()
    back_attend(chip)
    gather_out.wait_rest()
    back_attend(away)
    scatter_input = scatter(3, part)
    scatter_input.pre()
    turn_rows(rows_out, turned_more)
    scatter_input.across()
    scatter_input.local()
    sum_down.sum()

    weight_grad(3, (turned, flat(grad_projected)), (turned_more, flat(attended)))
    sum_attend = halving(3)
    sum_attend.send()

    grad_h = scatter_input.total()
    normed = norm_attend[...]
    grad_tokens[...] = (
        grad_middle[...] + norm_back(grad_h * (1.0 + mod(0)), normed, inverse_attend)
    ).astype(BF)
    keep_mod(0, grad_h * normed)
    keep_mod(1, grad_h)
    to_near = remote.start(mod_part, mod_near, near_device)

    stores = []

    def store(src, dst):
        copy = pltpu.make_async_copy(src, dst, store_sems.at[len(stores)])
        copy.start()
        stores.append(copy)

    store(result, result_out)
    store(grad_tokens, grad_tokens_out)

    sum_gate.sum()
    sum_down.sum()

    to_near.wait_recv()
    mod_sum[...] = mod_part[...] + mod_near[...]
    to_far = remote.start(mod_sum, mod_far, far_device)

    for sent in score_copies:
        for copy in sent:
            copy.wait_recv()
    store(scores_own, scores_out)

    def bias_grad_block(index, total):
        slot = lax.rem(index, PAIR_SLOTS)
        pair_copy(index).wait()
        for row_index in range(PAIR_ROWS):
            place_row = lax.rem(index, blocks) * PAIR_ROWS + row_index
            rows = jnp.concatenate(
                [
                    stage[half, pl.ds(place_row, 16, stride=queries_local), :].astype(BF)
                    for half in range(2)
                ],
                axis=1,
            )
            total = total + nn(rows, pair[slot, row_index])

        @pl.when(index + PAIR_SLOTS < n_blocks)
        def _():
            pair_copy(index + PAIR_SLOTS).start()

        return total

    total = jnp.zeros((16, pair_hbm.shape[3]), F32)
    for turn in range(2):
        chain = lax.rem(chip + turn, 2)
        for half in range(2):
            stage[half, 0:all_rows, :] = (
                scores_own[chain, :, :, half * 128 : (half + 1) * 128]
                .reshape(all_rows, 128)
                .astype(F32)
            )
            stage[half, all_rows:, :] = jnp.zeros((16 * queries_local - all_rows, 128), F32)
        total = lax.fori_loop(turn * blocks, (turn + 1) * blocks, bias_grad_block, total)
    bias_grads[0] = total
    tensor_copies = [
        remote.start(bias_grads.at[0], bias_grads.at[1 + index], device)
        for index, device in enumerate((near_device, far_device, cross_device))
    ]
    to_far.wait_recv()
    own, other = mod_sum[...], mod_far[...]
    low = jnp.where(chip == 0, own, other)
    high = jnp.where(chip == 0, other, own)
    mods_all[dp] = jnp.concatenate([low, high], axis=0).astype(BF)
    mod_copies = [
        remote.start(mods_all.at[dp], mods_all.at[dp], dp_device(lax.rem(dp + step, groups)))
        for step in range(1, groups)
    ]
    for copy in tensor_copies:
        copy.wait_recv()
    bias_sums[0] = bias_grads[0] + bias_grads[1] + bias_grads[2] + bias_grads[3]
    bias_copies = [
        remote.start(bias_sums.at[0], bias_sums.at[step], dp_device(lax.rem(dp + step, groups)))
        for step in range(1, groups)
    ]

    sum_up.sum()
    sum_gate.sum()
    final_weights[0] = sum_down.last()
    sum_attend.sum()
    sum_up.sum()
    final_weights[2] = sum_gate.last()
    for copy in hot_copies + mod_copies:
        copy.wait_recv()
    store(hots, hots_out)
    store(mods_all, mods_out)
    for copy in bias_copies:
        copy.wait_recv()
    bias_grad[...] = jnp.sum(bias_sums[...], axis=0)
    store(bias_grad, bias_grad_out)
    sum_attend.sum()
    final_weights[3] = sum_up.last()
    final_weights[1] = sum_attend.last()
    store(final_weights, weights_out)
    for copy in stores:
        copy.wait()
    remote.finish()


def finish_kernel(
    dims,
    result_in,
    grad_tokens_in,
    weights_hbm,
    scores_ref,
    mods_ref,
    hots_ref,
    bias_grad_ref,
    weights_ref,
    bias_ref,
    modulation_ref,
    time_ref,
    class_ref,
    result_out,
    grad_tokens_out,
    grad_pair_ref,
    grad_bias_ref,
    grad_input_ref,
    grad_output_ref,
    grad_hidden_out,
    grad_down_ref,
    grad_modulation_ref,
    grad_time_ref,
    grad_class_ref,
    stage,
    bias_turned,
    expanded,
    grad_condition,
    sems,
):
    (groups, chains, span, local, width, local_width, queries_local, hidden) = dims
    heads = local_width // HD
    step = pl.program_id(0)
    blocks = queries_local // PAIR_ROWS
    all_rows = 4 * heads * queries_local
    rows_all = groups * 16
    times = time_ref.shape[0]

    def copies():
        return [
            pltpu.make_async_copy(result_in, result_out, sems.at[0]),
            pltpu.make_async_copy(grad_tokens_in, grad_tokens_out, sems.at[1]),
            pltpu.make_async_copy(weights_hbm.at[2], grad_hidden_out.at[0], sems.at[2]),
            pltpu.make_async_copy(weights_hbm.at[3], grad_hidden_out.at[1], sems.at[3]),
        ]

    @pl.when(step == 0)
    def _():
        for copy in copies():
            copy.start()
        wide = jnp.concatenate(
            [
                bias_ref[...].astype(F32),
                jnp.zeros((bias_ref.shape[0], 128 - bias_ref.shape[1]), F32),
            ],
            axis=1,
        )
        bias_turned[...] = jnp.transpose(wide)[:16].astype(BF)
        for half in range(2):
            stage[half, all_rows:, :] = jnp.zeros((16 * queries_local - all_rows, 128), F32)
        hot = hots_ref[...].reshape(rows_all, hots_ref.shape[2])
        lane = lax.broadcasted_iota(jnp.int32, hot.shape, 1)
        zero = jnp.zeros_like(hot)
        expanded[0] = nn(jnp.where(lane < times, hot, zero)[:, :times], time_ref[...]).astype(BF)
        expanded[1] = nn(jnp.where(lane < times, zero, hot)[:, times:], class_ref[...]).astype(BF)
        grad_condition[...] = jnp.zeros_like(grad_condition)

    @pl.when(lax.rem(step, blocks) == 0)
    def _():
        chain = step // blocks
        for half in range(2):
            stage[half, 0:all_rows, :] = (
                scores_ref[chain, :, :, half * 128 : (half + 1) * 128]
                .reshape(all_rows, 128)
                .astype(F32)
            )

    @pl.when(step < 6)
    def _():
        member = lax.broadcasted_iota(jnp.int32, (rows_all, 1), 0)
        mine = jnp.where(lax.rem(member, 8) == step, 1.0, 0.0)
        rows = mods_ref[...].reshape(rows_all, width)
        time_rows = (expanded[0].astype(F32) * mine).astype(BF)
        class_rows = (expanded[1].astype(F32) * mine).astype(BF)
        grad_modulation_ref[...] = tn(time_rows, rows) + tn(class_rows, rows)
        grad_condition[...] += mine * nt(rows, modulation_ref[...])

    @pl.when(step == 6)
    def _():
        hot = hots_ref[...].reshape(rows_all, hots_ref.shape[2])
        rest = grad_condition[...]
        table = jnp.zeros((hot.shape[1], rest.shape[1]), F32)
        for _ in range(3):
            piece = rest.astype(BF)
            table = table + tn(hot, piece)
            rest = rest - piece.astype(F32)
        grad_time_ref[...] = table[:times]
        grad_class_ref[...] = table[times:]
        grad_bias_ref[...] = jnp.transpose(bias_grad_ref[...])[:, : 4 * heads]

    @pl.when(step == 7)
    def _():
        grad_down_ref[...] = jnp.transpose(weights_ref[0])
        for index in range(3):
            grad_input_ref[index] = weights_ref[1, :, index * local_width : (index + 1) * local_width]
        grad_output_ref[...] = jnp.transpose(weights_ref[1, :, 3 * local_width :])

    for row_index in range(PAIR_ROWS):
        place_row = lax.rem(step, blocks) * PAIR_ROWS + row_index
        rows = jnp.concatenate(
            [
                stage[half, pl.ds(place_row, 16, stride=queries_local), :].astype(BF)
                for half in range(2)
            ],
            axis=1,
        )
        grad_pair_ref[row_index] = tn(rows, bias_turned[...]).astype(BF)

    @pl.when(step == pl.num_programs(0) - 1)
    def _():
        for copy in copies():
            copy.wait()


def body(
    groups,
    tokens,
    pair_features,
    cotangent,
    chain_length,
    time_bin,
    cath_class,
    bias_weight,
    input_weight,
    output_weight,
    hidden_weight,
    down_weight,
    modulation_weight,
    time_table,
    class_table,
):
    chains, queries_local, span, channels = pair_features.shape
    local, width = tokens.shape
    local_width = input_weight.shape[2]
    hidden = down_weight.shape[0]
    heads = local_width // HD
    rows = chains * span
    chunk = width // groups
    assert chains == 2 and rows == 4 * local and span == 2 * local
    assert span == 256 and channels == 256 and 4 * local_width == width == hidden
    assert queries_local % PAIR_ROWS == 0
    dims = (groups, chains, span, local, width, local_width, queries_local, hidden)
    bits = groups.bit_length() - 1
    assert groups == 1 << bits
    straight = tuple(range(bits))
    orders = (straight, straight, straight, straight)
    n_table = time_table.shape[0] + class_table.shape[0]

    anywhere = pl.BlockSpec(memory_space=pl.ANY)
    scalars = pl.BlockSpec(memory_space=pltpu.SMEM)
    vmem = pltpu.VMEM
    half_rows = (chains, span, width)
    slots = (4, local, width)
    messages = 3 * 8 + 6 * 2 + 4 * bits + 3 * (groups - 1) + 5
    weights_shape = (4, chunk, width)
    outs = pl.pallas_call(
        functools.partial(layer_kernel, dims, orders),
        out_shape=(
            jax.ShapeDtypeStruct((local, width), BF),
            jax.ShapeDtypeStruct((local, width), BF),
            jax.ShapeDtypeStruct((chains, 4 * heads, queries_local, span), BF),
            jax.ShapeDtypeStruct((groups, 16, width), BF),
            jax.ShapeDtypeStruct((groups, 16, n_table), BF),
            jax.ShapeDtypeStruct((16, channels), F32),
            jax.ShapeDtypeStruct(weights_shape, F32),
        ),
        in_specs=[scalars] * 3 + [anywhere] * 11,
        out_specs=[anywhere] * 7,
        scratch_shapes=[
            vmem((local, width), BF),
            vmem((local, width), BF),
            vmem((PAIR_SLOTS, PAIR_ROWS, span, channels), BF),
            vmem(bias_weight.shape, BF),
            vmem(input_weight.shape, BF),
            vmem(output_weight.shape, BF),
            vmem(hidden_weight.shape, BF),
            vmem(down_weight.shape, BF),
            vmem(modulation_weight.shape, BF),
            vmem((n_table, time_table.shape[1]), BF),
            vmem((8, modulation_weight.shape[1]), F32),
            vmem((2, 16 * queries_local, 128), F32),
            vmem((groups, 16, n_table), BF),
            vmem((groups, 16, width), BF),
            vmem(slots, BF),
            vmem(slots, BF),
            vmem(slots, BF),
            vmem(slots, BF),
            vmem((chains, 4 * heads, queries_local, span), BF),
            vmem((chains, heads, span, span), BF),
            vmem((chains, span, local_width), BF),
            vmem((chains, span, local_width), BF),
            vmem((chains, span, local_width), BF),
            vmem((chains, heads * span, span), F32),
            vmem((chains, span, local_width), BF),
            vmem(slots, F32),
            vmem(slots, F32),
            vmem(half_rows, F32),
            vmem(half_rows, BF),
            vmem(half_rows, BF),
            vmem(half_rows, BF),
            vmem((chains, heads, span, span), BF),
            vmem((chains, 4 * heads, queries_local, span), BF),
            vmem((chains, span, 3 * local_width), BF),
            vmem((4, 3, local, width), BF),
            vmem((4, 3, local, width), BF),
            vmem((width, rows), BF),
            vmem((width, rows), BF),
            vmem((4, groups, chunk, width), BF),
            vmem((4, groups, chunk, width), BF),
            vmem(weights_shape, F32),
            vmem((local, width), F32),
            vmem((local, width), F32),
            vmem((local, width), F32),
            vmem((local, width), F32),
            vmem((local, width), F32),
            vmem((local, width), BF),
            vmem((local, width), BF),
            vmem((8, width), F32),
            vmem((8, width), F32),
            vmem((8, width), F32),
            vmem((8, width), F32),
            vmem((4, 16, channels), F32),
            vmem((groups, 16, channels), F32),
            vmem((16, channels), F32),
            pltpu.SemaphoreType.DMA((11,)),
            pltpu.SemaphoreType.DMA((PAIR_SLOTS,)),
            pltpu.SemaphoreType.DMA((8,)),
            pltpu.SemaphoreType.DMA((messages,)),
            pltpu.SemaphoreType.DMA((messages,)),
        ],
        compiler_params=pltpu.CompilerParams(
            collective_id=0, has_side_effects=True, vmem_limit_bytes=VMEM_BYTES
        ),
        name="layer",
    )(
        chain_length,
        time_bin,
        cath_class,
        tokens,
        cotangent,
        pair_features,
        bias_weight,
        input_weight,
        output_weight,
        hidden_weight,
        down_weight,
        modulation_weight,
        time_table,
        class_table,
    )
    result, grad_tokens, scores, mods_all, hots, bias_grad, weights = outs

    blocks = queries_local // PAIR_ROWS

    def whole(shape):
        return pl.BlockSpec(shape, lambda i: (0,) * len(shape))

    kept = weights
    sixth = modulation_weight.shape[1] // 6

    def by_vector(i):
        return (0, jnp.minimum(i, 5))

    outs = pl.pallas_call(
        functools.partial(finish_kernel, dims),
        grid=(chains * blocks,),
        out_shape=(
            jax.ShapeDtypeStruct((local, width), BF),
            jax.ShapeDtypeStruct((local, width), BF),
            jax.ShapeDtypeStruct(pair_features.shape, BF),
            jax.ShapeDtypeStruct(bias_weight.shape, F32),
            jax.ShapeDtypeStruct((3, chunk, local_width), F32),
            jax.ShapeDtypeStruct((local_width, chunk), F32),
            jax.ShapeDtypeStruct((2, chunk, hidden), F32),
            jax.ShapeDtypeStruct((hidden, chunk), F32),
            jax.ShapeDtypeStruct(modulation_weight.shape, F32),
            jax.ShapeDtypeStruct(time_table.shape, F32),
            jax.ShapeDtypeStruct(class_table.shape, F32),
        ),
        in_specs=[
            anywhere,
            anywhere,
            anywhere,
            whole(scores.shape),
            whole(mods_all.shape),
            whole(hots.shape),
            whole(bias_grad.shape),
            pl.BlockSpec((2, chunk, width), lambda i: (0, 0, 0)),
            whole(bias_weight.shape),
            pl.BlockSpec((modulation_weight.shape[0], sixth), by_vector),
            whole(time_table.shape),
            whole(class_table.shape),
        ],
        out_specs=[
            anywhere,
            anywhere,
            pl.BlockSpec(
                (None, PAIR_ROWS, span, channels), lambda i: (i // blocks, lax.rem(i, blocks), 0, 0)
            ),
            whole(bias_weight.shape),
            whole((3, chunk, local_width)),
            whole((local_width, chunk)),
            anywhere,
            whole((hidden, chunk)),
            pl.BlockSpec((modulation_weight.shape[0], sixth), by_vector),
            whole(time_table.shape),
            whole(class_table.shape),
        ],
        scratch_shapes=[
            vmem((2, 16 * queries_local, 128), F32),
            vmem((16, channels), BF),
            vmem((2, groups * 16, time_table.shape[1]), BF),
            vmem((groups * 16, time_table.shape[1]), F32),
            pltpu.SemaphoreType.DMA((4,)),
        ],
        compiler_params=pltpu.CompilerParams(vmem_limit_bytes=48 << 20),
        name="finish",
    )(
        result,
        grad_tokens,
        weights,
        scores,
        mods_all,
        hots,
        bias_grad,
        kept,
        bias_weight,
        modulation_weight,
        time_table,
        class_table,
    )
    return outs


def solution(mesh):
    placed = (
        P(("dp", "tensor"), None),
        P("dp", "tensor", None, None),
        P(("dp", "tensor"), None),
        P("dp"),
        P("dp"),
        P("dp"),
        P(),
        P(None, None, "tensor"),
        P("tensor", None),
        P(None, None, "tensor"),
        P("tensor", None),
        P(),
        P(),
        P(),
    )
    assert mesh.shape["tensor"] == 4
    return jax.shard_map(
        functools.partial(body, mesh.shape["dp"]),
        mesh=mesh,
        in_specs=placed,
        out_specs=(
            P(("dp", "tensor"), None),
            P(("dp", "tensor"), None),
            P("dp", "tensor", None, None),
            P(),
            P(None, "dp", "tensor"),
            P("tensor", "dp"),
            P(None, "dp", "tensor"),
            P("tensor", "dp"),
            P(),
            P(),
            P(),
        ),
        check_vma=False,
    )
```

time: 594 us -> 144 us (0.24)
  waiting for transfers between devices: 247 us -> 0 us
  blocking collectives: 176 us -> 0 us
  Pallas kernels: 0 us -> 129 us
  matrix products: 72.9 us -> 0 us
  local copies, waits for them, and re-layouts: 55.4 us -> 12 us
  other arithmetic: 17.9 us -> 0 us
  between operations: 15.5 us -> 0.71 us
  starting transfers between devices: 8.25 us -> 0 us
    reduce_scatter x5 -> x0, waiting for transfers between devices: 138 us -> none  [the longest x1 70.1 us: body(): lax.psum_scatter(grad_down, 'dp', scatter_dimension=1, tiled=True)]
    pallas_call x0 -> x2, Pallas kernels: none -> 129 us  [the longest x1 117 us: body(): pl.pallas_call(functools.partial(layer_kernel, dims, orders), out_shape=(...]
    all_gather x8 -> x0, blocking collectives: 121 us -> none  [the longest x1 31 us: body(): lax.all_gather(chain_mods.astype(jnp.bfloat16), 'dp', axis=0, tiled=True)]
    unnamed x11 -> x0, waiting for transfers between devices: 109 us -> none
    dot_general x28 -> x0, matrix products: 70.9 us -> none  [the longest x1 11.4 us: body(): jnp.einsum('cijp,ph->chij', pair_features, bias_weight, preferred_element...]
    psum x2 -> x0, blocking collectives: 54.6 us -> none  [the longest x1 43 us: body(): bias_total = lax.psum(grad_bias_w, ('dp', 'tensor'))]
    unnamed x141 -> x24, local copies, waits for them, and re-layouts: 28.9 us -> 10.4 us
    convert_element_type x5 -> x0, local copies, waits for them, and re-layouts: 8.69 us -> none  [the longest x2 4.3 us: scores_of(): bias_full.astype(jnp.float32)]
  transfers between devices with their start and end apart: 10 -> 0, of which waited for: 6 -> 0; matrix products, arithmetic and copies ran while one was open for 17% -> 0% of each run, Pallas kernels for 0% -> 0%
where the time goes in v1:
time: 144 us; the launch traced here: 142 us
  Pallas kernels  129 us (90%)
  local copies, waits for them, and re-layouts  12 us (8%)
    pallas_call x1, Pallas kernels, body(): pl.pallas_call(functools.partial(layer_kernel, dims, orders), out_shape=(...  117 us
    pallas_call x1, Pallas kernels, body(): pl.pallas_call(functools.partial(finish_kernel, dims), grid=(chains * blo...  12.8 us
    unnamed x24, local copies, waits for them, and re-layouts  10.4 us

profile of v1, /device:TPU:0, one launch (start us, length us, event | category | flops | bytes accessed | tf_op | source)
XLA Modules:
  0.0 142.0 jit_solution(15116557553804072483)
XLA Ops:
  0.6 1.4 %copy.25.bias_hbm.bias_ref = bf16[256,12]{1,0:T(8,128)(2,1)} copy(bf16[256,12]{0,1:T(8,128)(2,1)} %param.20) | data formatting | bytes 12288 | tf_op args[6]
  2.1 2.3 %copy.26.input_hbm = bf16[3,768,192]{2,1,0:T(8,128)(2,1)} copy(bf16[3,768,192]{1,2,0:T(8,128)(2,1)} %param.21) | data formatting | bytes 1769472 | tf_op args[7]
  4.4 0.0 copy-start
  4.4 0.0 copy-start.3
  4.4 0.0 copy-start.7
  4.4 0.0 copy-start.8
  4.4 116.5 %layer.1 = (bf16[128,768]{1,0:T(8,128)(2,1)}, bf16[128,768]{1,0:T(8,128)(2,1)}, bf16[2,12,64,256]{3,2,1,0:T(8,128)(2,1)}, bf16[8,16,768]{2,1,0:T(8,128)(2,1)}, b...) custom-call(s32[2]{0:T(128)} %length_ref.1, s32[2]{0:T(128)} %time_ref.2, s32[2]{0:T(128)} %class_ref.2, ...), custom_call_target="tpu_custom_call" | custom-call | tf_op jit(solution)/shard_map/layer/pallas_call | solution.py:939
  121.0 0.0 copy-done
  121.0 0.0 copy-done.3
  121.0 0.0 copy-done.7
  121.0 0.0 copy-done.8
  121.0 0.0 copy-start.1
  121.0 1.3 copy-done.1
  122.3 0.0 copy-start.2
  122.3 1.1 copy-done.2
  123.4 0.0 copy-start.4
  123.4 0.9 copy-done.4
  124.3 0.9 copy-done.5
  125.3 0.9 copy-done.6
  126.2 0.8 copy-done.9
  126.9 0.7 copy-done.10
  127.7 12.8 %finish.1 = (bf16[128,768]{1,0:T(8,128)(2,1)}, bf16[128,768]{1,0:T(8,128)(2,1)}, bf16[2,64,256,256]{3,2,1,0:T(8,128)(2,1)}, f32[256,12]{1,0:T(8,128)S(1)}, f32[3...) custom-call(bf16[128,768]{1,0:T(8,128)(2,1)S(1)} %copy-done.4, ...), custom_call_target="tpu_custom_call" | custom-call | tf_op jit(solution)/shard_map/finish/pallas_call | solution.py:1047
  140.5 0.7 copy.28
  141.1 0.9 copy.29
  (4 shorter events, 0.0 us)
Async XLA Ops:
  4.4 116.6 %copy-start = (bf16[256,4608]{1,0:T(8,128)(2,1)S(1)}, bf16[256,4608]{1,0:T(8,128)(2,1)}, u32[]{:S(2)}) copy-start(bf16[256,4608]{1,0:T(8,128)(2,1)} %modulation_ref.1) | copy-start | bytes 7077892
  4.4 116.6 %copy-start.3 = (bf16[256,12]{1,0:T(8,128)(2,1)S(1)}, bf16[256,12]{1,0:T(8,128)(2,1)}, u32[]{:S(2)}) copy-start(bf16[256,12]{1,0:T(8,128)(2,1)} %copy.25.bias_hbm.bias_ref) | copy-start | bytes 18436
  4.4 116.6 %copy-start.7 = (bf16[64,256]{1,0:T(8,128)(2,1)S(1)}, bf16[64,256]{1,0:T(8,128)(2,1)}, u32[]{:S(2)}) copy-start(bf16[64,256]{1,0:T(8,128)(2,1)} %time_ref.3) | copy-start | bytes 98308
  4.4 116.6 %copy-start.8 = (bf16[64,256]{1,0:T(8,128)(2,1)S(1)}, bf16[64,256]{1,0:T(8,128)(2,1)}, u32[]{:S(2)}) copy-start(bf16[64,256]{1,0:T(8,128)(2,1)} %class_ref.3) | copy-start | bytes 98308
  121.0 1.3 copy-start.1
  122.3 1.1 copy-start.2
  123.4 0.9 copy-start.4
  124.3 0.9 copy-start.5
  125.3 0.9 copy-start.6
  126.2 0.8 copy-start.9
  126.9 0.7 copy-start.10

commit v2 on v1

--- a/solution.py
+++ b/solution.py
@@ -15,6 +15,17 @@
 PAIR_SLOTS = 4
 PAIR_ROWS = 16
 VMEM_BYTES = 60 << 20
+PIECES = (
+    (0, 0, 384, 2),
+    (0, 384, 384, 2),
+    (2, 0, 384, 0),
+    (2, 384, 384, 0),
+    (3, 0, 384, 0),
+    (3, 384, 384, 0),
+    (1, 0, 256, 0),
+    (1, 256, 256, 0),
+    (1, 512, 256, 0),
+)
 
 
 def nn(a, b):
@@ -143,16 +154,20 @@
         self.landing += self.half
         self.step += 1
         if self.step == len(self.order):
-            return total[0]
+            self.result = total[0]
+            return
         self.store[keep] = total.astype(BF)
         self.send()
-        return None
-
-    def last(self):
-        total = None
-        while total is None:
-            total = self.sum()
-        return total
+
+    def finish(self):
+        while self.step < len(self.order):
+            self.sum()
+        return self.result
+
+
+def padded(rows):
+    more = jnp.zeros((16 - rows.shape[0], rows.shape[1]), F32)
+    return jnp.concatenate([rows.astype(F32), more], axis=0).astype(BF)
 
 
 def slot_of(chunk, order):
@@ -183,7 +198,8 @@
     grad_tokens_out,
     scores_out,
     mods_out,
-    hots_out,
+    expanded_out,
+    tables_out,
     bias_grad_out,
     weights_out,
     tokens,
@@ -224,8 +240,6 @@
     scatter_recv,
     turned,
     turned_more,
-    grad_store,
-    grad_recv,
     final_weights,
     norm_attend,
     norm_hidden,
@@ -241,12 +255,16 @@
     bias_grads,
     bias_sums,
     bias_grad,
+    expanded,
+    tables_grad,
     load_sems,
     pair_sems,
     store_sems,
     send_sems,
     recv_sems,
+    *piece_refs,
 ):
+    piece_store, piece_recv = piece_refs[: len(PIECES)], piece_refs[len(PIECES) :]
     (groups, chains, span, local, width, local_width, queries_local, hidden) = dims
     heads = local_width // HD
     dp = lax.axis_index("dp")
@@ -297,12 +315,7 @@
     load_modulation = load(modulation_hbm, modulation_weight)
     load_cotangent = load(cotangent_hbm, cotangent)
     load_bias = load(bias_hbm, bias_weight)
-    for index in range(PAIR_SLOTS):
-        pair_copy(index).start()
-    load_input = load(input_hbm, input_weight)
-    load_output = load(output_hbm, output_weight)
-    load_down = load(down_hbm, down_weight)
-    load_hidden = load(hidden_hbm, hidden_weight)
+    pair_copy(0).start()
 
     remote = Remote(send_sems, recv_sems)
 
@@ -319,6 +332,9 @@
     load_class.wait()
     condition = nn(jnp.where(picked, 1.0, 0.0).astype(BF), tables[...]).astype(BF)
     load_modulation.wait()
+    for index in range(1, PAIR_SLOTS):
+        pair_copy(index).start()
+    load_input = load(input_hbm, input_weight)
     both = nn(condition, modulation_weight[...])
     mods[...] = jnp.broadcast_to(both[0:1] + both[1:2], mods.shape)
 
@@ -336,14 +352,7 @@
     gate_hidden = sigmoid(mod(5))
     rows_down[me] = (cotangent[...].astype(F32) * valid * gate_hidden).astype(BF)
     load_bias.wait()
-    wide = jnp.concatenate(
-        [
-            bias_weight[...].astype(F32),
-            jnp.zeros((bias_weight.shape[0], 128 - bias_weight.shape[1]), F32),
-        ],
-        axis=1,
-    )
-    bias_turned = jnp.transpose(wide)[:16].astype(BF)
+    bias_rows = padded(bias_weight[...])
 
     pl.semaphore_wait(barrier, 3 + groups - 1)
     gather_attend = Gather(remote, rows_attend, me, near, far, near_device, far_device)
@@ -356,7 +365,7 @@
         slot = lax.rem(index, PAIR_SLOTS)
         pair_copy(index).wait()
         for row_index in range(PAIR_ROWS):
-            product = nt(bias_turned, pair[slot, row_index])
+            product = nt(bias_rows, pair[slot, row_index])
             place_row = lax.rem(index, blocks) * PAIR_ROWS + row_index
             for half in range(2):
                 stage[half, pl.ds(place_row, 16, stride=queries_local), :] = product[
@@ -392,6 +401,11 @@
         bias_full[chain, :, mine, :] = bias_send[chain, pl.ds(me * heads, heads)]
         if turn == 0:
             gather_attend.forward()
+            load_output = load(output_hbm, output_weight)
+            load_down = load(down_hbm, down_weight)
+            load_hidden = load(hidden_hbm, hidden_weight)
+
+    gather_down = Gather(remote, rows_down, me, near, far, near_device, far_device)
 
     for index in range(PAIR_SLOTS):
         pair_copy(index).start()
@@ -400,9 +414,9 @@
 
     def project(half):
         rows = rows_attend[pl.ds(2 * half, 2)].reshape(span, width)
-        queries[half] = nn(rows, input_weight[0]).astype(BF)
-        keys[half] = nn(rows, input_weight[1]).astype(BF)
-        values[half] = nn(rows, input_weight[2]).astype(BF)
+        queries[half] = nt(rows, input_weight[0]).astype(BF)
+        keys[half] = nt(rows, input_weight[1]).astype(BF)
+        values[half] = nt(rows, input_weight[2]).astype(BF)
 
     gather_attend.wait_near()
     project(chip)
@@ -470,7 +484,6 @@
     bias_copies[1][1].wait_recv()
     bias_copies[0][2].wait_recv()
     scatter_attend.across()
-    gather_down = Gather(remote, rows_down, me, near, far, near_device, far_device)
     attend(chip)
     put(part, chip, nn(attended[chip], output_weight[...]))
     scatter_attend.local()
@@ -486,9 +499,11 @@
                 rows[slot * local : (slot + 1) * local]
             )
 
+    gather_down.forward()
     gather_down.wait_near()
     back_down(chip)
-    gather_down.forward()
+    gather_down.wait_rest()
+    back_down(away)
 
     gate_attend = sigmoid(mod(2))
     out_total = scatter_attend.total()
@@ -499,8 +514,6 @@
     norm_hidden[...] = normed
     rows_hidden[me] = (normed * (1.0 + mod(3)) + mod(4)).astype(BF)
     gather_hidden = Gather(remote, rows_hidden, me, near, far, near_device, far_device)
-    gather_down.wait_rest()
-    back_down(away)
 
     load_hidden.wait()
 
@@ -522,6 +535,50 @@
             nt(grad_gate[half], hidden_weight[0]) + nt(grad_up[half], hidden_weight[1]),
         )
 
+    chunk = width // groups
+    per_block = max(1, 192 // chunk)
+
+    def weight_grad(pieces, *pairs):
+        for block in range(groups // per_block):
+            rows = slice(block * per_block * chunk, (block + 1) * per_block * chunk)
+            product = jnp.concatenate([nn(left[rows, :], right) for left, right in pairs], axis=1)
+            for index in pieces:
+                first, size = PIECES[index][1:3]
+                for inner in range(per_block):
+                    slot = slot_of(block * per_block + inner, orders[index])
+                    piece_store[index][slot] = product[
+                        inner * chunk : (inner + 1) * chunk, first : first + size
+                    ].astype(BF)
+        for index in pieces:
+            sums[index] = Halving(
+                remote,
+                piece_store[index],
+                piece_recv[index],
+                dp,
+                groups,
+                dp_device,
+                orders[index],
+            )
+            sums[index].send()
+
+    sums = {}
+
+    def advance(*indices):
+        for index in indices:
+            sums[index].sum()
+
+    def complete(*indices):
+        for index in indices:
+            matrix, first, size = PIECES[index][:3]
+            final_weights[matrix, :, first : first + size] = sums[index].finish()
+
+    def flat(ref):
+        return ref[...].reshape(chains * span, ref.shape[-1])
+
+    def turn_rows(source, target):
+        for slot in range(4):
+            target[:, slot * local : (slot + 1) * local] = jnp.transpose(source[slot])
+
     gather_hidden.wait_near()
     transition(chip)
     gather_hidden.forward()
@@ -529,6 +586,7 @@
     put(part_down, chip, nn(active[chip], down_weight[...]))
     gather_hidden.wait_rest()
     transition(away)
+    weight_grad((0, 1), (turned, flat(active)))
     back_hidden(away)
     scatter_hidden = scatter(1, part)
     scatter_hidden.pre()
@@ -538,48 +596,10 @@
     scatter_down = scatter(2, part_down)
     scatter_down.pre()
 
-    chunk = width // groups
-    per_block = max(1, 192 // chunk)
-
-    def halving(index):
-        return Halving(
-            remote,
-            grad_store.at[index],
-            grad_recv.at[index],
-            dp,
-            groups,
-            dp_device,
-            orders[index],
-        )
-
-    def weight_grad(index, *pairs):
-        for block in range(groups // per_block):
-            rows = slice(block * per_block * chunk, (block + 1) * per_block * chunk)
-            product = jnp.concatenate([nn(left[rows, :], right) for left, right in pairs], axis=1)
-            for inner in range(per_block):
-                grad_store[index, slot_of(block * per_block + inner, orders[index])] = product[
-                    inner * chunk : (inner + 1) * chunk
-                ].astype(BF)
-
-    def flat(ref):
-        return ref[...].reshape(chains * span, ref.shape[-1])
-
-    def turn_rows(source, target):
-        for slot in range(4):
-            target[:, slot * local : (slot + 1) * local] = jnp.transpose(source[slot])
-
-    weight_grad(0, (turned, flat(active)))
-    sum_down = halving(0)
-    sum_down.send()
     scatter_down.across()
     scatter_down.local()
     turn_rows(rows_hidden, turned_more)
-    weight_grad(1, (turned_more, flat(grad_gate)))
-    sum_gate = halving(1)
-    sum_gate.send()
-    weight_grad(2, (turned_more, flat(grad_up)))
-    sum_up = halving(2)
-    sum_up.send()
+    weight_grad((2, 3), (turned_more, flat(grad_gate)))
 
     grad_h = scatter_hidden.total()
     normed = norm_hidden[...]
@@ -587,6 +607,8 @@
     grad_middle[...] = back
     rows_out[me] = (back * valid * gate_attend).astype(BF)
     gather_out = Gather(remote, rows_out, me, near, far, near_device, far_device)
+
+    weight_grad((4, 5), (turned_more, flat(grad_up)))
 
     def keep_mod(index, rows):
         mod_part[index : index + 1, :] = jnp.sum(rows, axis=0, keepdims=True)
@@ -642,14 +664,15 @@
         put(
             part,
             chain,
-            nt(grad_query, input_weight[0])
-            + nt(grad_key, input_weight[1])
-            + nt(grad_value, input_weight[2]),
+            nn(grad_query, input_weight[0])
+            + nn(grad_key, input_weight[1])
+            + nn(grad_value, input_weight[2]),
         )
 
     gather_out.wait_near()
     gather_out.forward()
     back_attend(chip)
+    advance(0, 2)
     gather_out.wait_rest()
     back_attend(away)
     scatter_input = scatter(3, part)
@@ -657,21 +680,8 @@
     turn_rows(rows_out, turned_more)
     scatter_input.across()
     scatter_input.local()
-    sum_down.sum()
-
-    weight_grad(3, (turned, flat(grad_projected)), (turned_more, flat(attended)))
-    sum_attend = halving(3)
-    sum_attend.send()
-
-    grad_h = scatter_input.total()
-    normed = norm_attend[...]
-    grad_tokens[...] = (
-        grad_middle[...] + norm_back(grad_h * (1.0 + mod(0)), normed, inverse_attend)
-    ).astype(BF)
-    keep_mod(0, grad_h * normed)
-    keep_mod(1, grad_h)
-    to_near = remote.start(mod_part, mod_near, near_device)
-
+    weight_grad((6, 7, 8), (turned, flat(grad_projected)), (turned_more, flat(attended)))
+    advance(1, 3)
     stores = []
 
     def store(src, dst):
@@ -679,21 +689,10 @@
         copy.start()
         stores.append(copy)
 
-    store(result, result_out)
-    store(grad_tokens, grad_tokens_out)
-
-    sum_gate.sum()
-    sum_down.sum()
-
-    to_near.wait_recv()
-    mod_sum[...] = mod_part[...] + mod_near[...]
-    to_far = remote.start(mod_sum, mod_far, far_device)
-
     for sent in score_copies:
         for copy in sent:
             copy.wait_recv()
     store(scores_own, scores_out)
-
     def bias_grad_block(index, total):
         slot = lax.rem(index, PAIR_SLOTS)
         pair_copy(index).wait()
@@ -714,8 +713,7 @@
 
         return total
 
-    total = jnp.zeros((16, pair_hbm.shape[3]), F32)
-    for turn in range(2):
+    def bias_grad_chain(turn, total):
         chain = lax.rem(chip + turn, 2)
         for half in range(2):
             stage[half, 0:all_rows, :] = (
@@ -724,12 +722,41 @@
                 .astype(F32)
             )
             stage[half, all_rows:, :] = jnp.zeros((16 * queries_local - all_rows, 128), F32)
-        total = lax.fori_loop(turn * blocks, (turn + 1) * blocks, bias_grad_block, total)
-    bias_grads[0] = total
+        return lax.fori_loop(turn * blocks, (turn + 1) * blocks, bias_grad_block, total)
+
+    total = bias_grad_chain(0, jnp.zeros((16, pair_hbm.shape[3]), F32))
+    advance(0, 2, 4)
+    bias_grads[0] = bias_grad_chain(1, total)
     tensor_copies = [
         remote.start(bias_grads.at[0], bias_grads.at[1 + index], device)
         for index, device in enumerate((near_device, far_device, cross_device))
     ]
+
+    grad_h = scatter_input.total()
+    normed = norm_attend[...]
+    grad_tokens[...] = (
+        grad_middle[...] + norm_back(grad_h * (1.0 + mod(0)), normed, inverse_attend)
+    ).astype(BF)
+    keep_mod(0, grad_h * normed)
+    keep_mod(1, grad_h)
+    to_near = remote.start(mod_part, mod_near, near_device)
+
+    store(result, result_out)
+    store(grad_tokens, grad_tokens_out)
+
+    advance(1, 3)
+
+    to_near.wait_recv()
+    mod_sum[...] = mod_part[...] + mod_near[...]
+    to_far = remote.start(mod_sum, mod_far, far_device)
+    for copy in tensor_copies:
+        copy.wait_recv()
+    bias_sums[0] = bias_grads[0] + bias_grads[1] + bias_grads[2] + bias_grads[3]
+    bias_copies = [
+        remote.start(bias_sums.at[0], bias_sums.at[step], dp_device(lax.rem(dp + step, groups)))
+        for step in range(1, groups)
+    ]
+    advance(5)
     to_far.wait_recv()
     own, other = mod_sum[...], mod_far[...]
     low = jnp.where(chip == 0, own, other)
@@ -739,32 +766,53 @@
         remote.start(mods_all.at[dp], mods_all.at[dp], dp_device(lax.rem(dp + step, groups)))
         for step in range(1, groups)
     ]
-    for copy in tensor_copies:
+    complete(2)
+    advance(4, 6)
+    complete(3)
+    store(final_weights.at[2], weights_out.at[2])
+    for copy in hot_copies:
         copy.wait_recv()
-    bias_sums[0] = bias_grads[0] + bias_grads[1] + bias_grads[2] + bias_grads[3]
-    bias_copies = [
-        remote.start(bias_sums.at[0], bias_sums.at[step], dp_device(lax.rem(dp + step, groups)))
-        for step in range(1, groups)
-    ]
-
-    sum_up.sum()
-    sum_gate.sum()
-    final_weights[0] = sum_down.last()
-    sum_attend.sum()
-    sum_up.sum()
-    final_weights[2] = sum_gate.last()
-    for copy in hot_copies + mod_copies:
+    rows_all = groups * 16
+    hot = hots[...].reshape(rows_all, n_table)
+    hot_lane = lax.broadcasted_iota(jnp.int32, hot.shape, 1)
+    zero = jnp.zeros_like(hot)
+    time_rows = nn(jnp.where(hot_lane < times, hot, zero), tables[...])
+    class_rows = nn(jnp.where(hot_lane < times, zero, hot), tables[...])
+    expanded[:, :rows_all] = jnp.transpose(time_rows)
+    expanded[:, rows_all:] = jnp.transpose(class_rows)
+    store(expanded, expanded_out)
+    advance(5, 7)
+    complete(4)
+    advance(6, 8)
+    for copy in mod_copies:
         copy.wait_recv()
-    store(hots, hots_out)
     store(mods_all, mods_out)
+    rows = mods_all[...].reshape(rows_all, width)
+    member = lax.rem(lax.broadcasted_iota(jnp.int32, (rows_all, 1), 0), 8)
+    rest = jnp.zeros((rows_all, tables.shape[1]), F32)
+    for vector in range(6):
+        product = nt(rows, modulation_weight[:, vector * width : (vector + 1) * width])
+        rest = rest + jnp.where(member == vector, product, 0.0)
+    table = jnp.zeros((n_table, tables.shape[1]), F32)
+    for _ in range(3):
+        piece = rest.astype(BF)
+        table = table + tn(hot, piece)
+        rest = rest - piece.astype(F32)
+    tables_grad[...] = table
+    store(tables_grad, tables_out)
+    complete(0, 5)
+    store(final_weights.at[3], weights_out.at[3])
+    advance(7)
+    complete(1)
+    store(final_weights.at[0], weights_out.at[0])
     for copy in bias_copies:
         copy.wait_recv()
     bias_grad[...] = jnp.sum(bias_sums[...], axis=0)
     store(bias_grad, bias_grad_out)
-    sum_attend.sum()
-    final_weights[3] = sum_up.last()
-    final_weights[1] = sum_attend.last()
-    store(final_weights, weights_out)
+    complete(6)
+    advance(8)
+    complete(7, 8)
+    store(final_weights.at[1], weights_out.at[1])
     for copy in stores:
         copy.wait()
     remote.finish()
@@ -772,127 +820,143 @@
 
 def finish_kernel(
     dims,
-    result_in,
-    grad_tokens_in,
+    result_hbm,
+    grad_tokens_hbm,
     weights_hbm,
-    scores_ref,
-    mods_ref,
-    hots_ref,
-    bias_grad_ref,
-    weights_ref,
-    bias_ref,
-    modulation_ref,
-    time_ref,
-    class_ref,
+    scores_hbm,
+    mods_hbm,
+    expanded_hbm,
+    tables_hbm,
+    bias_grad_hbm,
+    bias_hbm,
     result_out,
     grad_tokens_out,
-    grad_pair_ref,
-    grad_bias_ref,
-    grad_input_ref,
-    grad_output_ref,
-    grad_hidden_out,
-    grad_down_ref,
-    grad_modulation_ref,
-    grad_time_ref,
-    grad_class_ref,
-    stage,
-    bias_turned,
+    pair_out,
+    bias_grad_out,
+    input_out,
+    output_out,
+    hidden_out,
+    down_out,
+    modulation_out,
+    time_out,
+    class_out,
+    rows_pass,
+    weights,
+    scores,
+    mods,
     expanded,
-    grad_condition,
-    sems,
+    tables,
+    bias_grad,
+    bias,
+    places,
+    pair,
+    modulation,
+    input_grad,
+    output_grad,
+    bias_rows,
+    load_sems,
+    pair_sems,
+    store_sems,
 ):
     (groups, chains, span, local, width, local_width, queries_local, hidden) = dims
     heads = local_width // HD
-    step = pl.program_id(0)
     blocks = queries_local // PAIR_ROWS
-    all_rows = 4 * heads * queries_local
-    rows_all = groups * 16
-    times = time_ref.shape[0]
-
-    def copies():
-        return [
-            pltpu.make_async_copy(result_in, result_out, sems.at[0]),
-            pltpu.make_async_copy(grad_tokens_in, grad_tokens_out, sems.at[1]),
-            pltpu.make_async_copy(weights_hbm.at[2], grad_hidden_out.at[0], sems.at[2]),
-            pltpu.make_async_copy(weights_hbm.at[3], grad_hidden_out.at[1], sems.at[3]),
-        ]
-
-    @pl.when(step == 0)
-    def _():
-        for copy in copies():
-            copy.start()
-        wide = jnp.concatenate(
-            [
-                bias_ref[...].astype(F32),
-                jnp.zeros((bias_ref.shape[0], 128 - bias_ref.shape[1]), F32),
+    times = time_out.shape[0]
+
+    def start(src, dst, semaphore):
+        copy = pltpu.make_async_copy(src, dst, semaphore)
+        copy.start()
+        return copy
+
+    moves = (
+        (bias_hbm, bias),
+        (scores_hbm.at[0], scores.at[0]),
+        (scores_hbm.at[1], scores.at[1]),
+        (expanded_hbm, expanded),
+        (mods_hbm, mods),
+        (weights_hbm, weights),
+        (result_hbm, rows_pass.at[0]),
+        (grad_tokens_hbm, rows_pass.at[1]),
+        (tables_hbm, tables),
+        (bias_grad_hbm, bias_grad),
+    )
+    loads = [start(src, dst, load_sems.at[index]) for index, (src, dst) in enumerate(moves)]
+
+    loads[0].wait()
+    weight_rows = bias[...].astype(F32)
+    spread = jnp.concatenate(
+        [
+            jnp.broadcast_to(weight_rows[head : head + 1], (PAIR_ROWS, weight_rows.shape[1]))
+            for head in range(4 * heads)
+        ],
+        axis=0,
+    )
+    member = lax.rem(lax.broadcasted_iota(jnp.int32, spread.shape, 0), PAIR_ROWS)
+    for row_index in range(PAIR_ROWS):
+        places[row_index] = jnp.where(member == row_index, spread, 0.0).astype(BF)
+
+    def pair_copy(index):
+        slot = lax.rem(index, PAIR_SLOTS)
+        return pltpu.make_async_copy(
+            pair.at[slot],
+            pair_out.at[
+                index // blocks, pl.ds(lax.rem(index, blocks) * PAIR_ROWS, PAIR_ROWS)
             ],
-            axis=1,
+            pair_sems.at[slot],
         )
-        bias_turned[...] = jnp.transpose(wide)[:16].astype(BF)
-        for half in range(2):
-            stage[half, all_rows:, :] = jnp.zeros((16 * queries_local - all_rows, 128), F32)
-        hot = hots_ref[...].reshape(rows_all, hots_ref.shape[2])
-        lane = lax.broadcasted_iota(jnp.int32, hot.shape, 1)
-        zero = jnp.zeros_like(hot)
-        expanded[0] = nn(jnp.where(lane < times, hot, zero)[:, :times], time_ref[...]).astype(BF)
-        expanded[1] = nn(jnp.where(lane < times, zero, hot)[:, times:], class_ref[...]).astype(BF)
-        grad_condition[...] = jnp.zeros_like(grad_condition)
-
-    @pl.when(lax.rem(step, blocks) == 0)
-    def _():
-        chain = step // blocks
-        for half in range(2):
-            stage[half, 0:all_rows, :] = (
-                scores_ref[chain, :, :, half * 128 : (half + 1) * 128]
-                .reshape(all_rows, 128)
-                .astype(F32)
-            )
-
-    @pl.when(step < 6)
-    def _():
-        member = lax.broadcasted_iota(jnp.int32, (rows_all, 1), 0)
-        mine = jnp.where(lax.rem(member, 8) == step, 1.0, 0.0)
-        rows = mods_ref[...].reshape(rows_all, width)
-        time_rows = (expanded[0].astype(F32) * mine).astype(BF)
-        class_rows = (expanded[1].astype(F32) * mine).astype(BF)
-        grad_modulation_ref[...] = tn(time_rows, rows) + tn(class_rows, rows)
-        grad_condition[...] += mine * nt(rows, modulation_ref[...])
-
-    @pl.when(step == 6)
-    def _():
-        hot = hots_ref[...].reshape(rows_all, hots_ref.shape[2])
-        rest = grad_condition[...]
-        table = jnp.zeros((hot.shape[1], rest.shape[1]), F32)
-        for _ in range(3):
-            piece = rest.astype(BF)
-            table = table + tn(hot, piece)
-            rest = rest - piece.astype(F32)
-        grad_time_ref[...] = table[:times]
-        grad_class_ref[...] = table[times:]
-        grad_bias_ref[...] = jnp.transpose(bias_grad_ref[...])[:, : 4 * heads]
-
-    @pl.when(step == 7)
-    def _():
-        grad_down_ref[...] = jnp.transpose(weights_ref[0])
-        for index in range(3):
-            grad_input_ref[index] = weights_ref[1, :, index * local_width : (index + 1) * local_width]
-        grad_output_ref[...] = jnp.transpose(weights_ref[1, :, 3 * local_width :])
-
-    for row_index in range(PAIR_ROWS):
-        place_row = lax.rem(step, blocks) * PAIR_ROWS + row_index
-        rows = jnp.concatenate(
-            [
-                stage[half, pl.ds(place_row, 16, stride=queries_local), :].astype(BF)
-                for half in range(2)
-            ],
-            axis=1,
-        )
-        grad_pair_ref[row_index] = tn(rows, bias_turned[...]).astype(BF)
-
-    @pl.when(step == pl.num_programs(0) - 1)
-    def _():
-        for copy in copies():
-            copy.wait()
+
+    def pair_block(index, carry):
+        @pl.when(index >= PAIR_SLOTS)
+        def _():
+            pair_copy(index - PAIR_SLOTS).wait()
+
+        rows = scores[index // blocks, :, pl.ds(lax.rem(index, blocks) * PAIR_ROWS, PAIR_ROWS)]
+        across = jnp.transpose(rows.reshape(4 * heads * PAIR_ROWS, rows.shape[2]))
+        slot = lax.rem(index, PAIR_SLOTS)
+        for row_index in range(PAIR_ROWS):
+            pair[slot, row_index] = nn(across, places[row_index]).astype(BF)
+        pair_copy(index).start()
+        return carry
+
+    n_blocks = chains * blocks
+    loads[1].wait()
+    loads[2].wait()
+    lax.fori_loop(0, n_blocks, pair_block, 0)
+
+    stores = []
+
+    def store(src, dst):
+        stores.append(start(src, dst, store_sems.at[len(stores)]))
+
+    loads[3].wait()
+    loads[4].wait()
+    rows = mods[...].reshape(groups * 16, width)
+    both = jnp.concatenate([rows, rows], axis=0)
+    lane = lax.rem(lax.broadcasted_iota(jnp.int32, expanded.shape, 1), 8)
+    for vector in range(6):
+        left = jnp.where(lane == vector, expanded[...], 0.0).astype(BF)
+        modulation[vector] = nn(left, both)
+        store(modulation.at[vector], modulation_out.at[:, pl.ds(vector * width, width)])
+    for copy in loads[5:]:
+        copy.wait()
+    store(weights.at[0], down_out)
+    store(weights.at[2], hidden_out.at[0])
+    store(weights.at[3], hidden_out.at[1])
+    store(rows_pass.at[0], result_out)
+    store(rows_pass.at[1], grad_tokens_out)
+    store(tables.at[pl.ds(0, times)], time_out)
+    store(tables.at[pl.ds(times, class_out.shape[0])], class_out)
+    bias_rows[...] = bias_grad[: 4 * heads]
+    store(bias_rows, bias_grad_out)
+    for index in range(3):
+        input_grad[index] = weights[1, :, index * local_width : (index + 1) * local_width]
+    store(input_grad, input_out)
+    output_grad[...] = jnp.transpose(weights[1, :, 3 * local_width :])
+    store(output_grad, output_out)
+    for index in range(n_blocks - PAIR_SLOTS, n_blocks):
+        pair_copy(index).wait()
+    for copy in stores:
+        copy.wait()
 
 
 def body(
@@ -926,15 +990,18 @@
     bits = groups.bit_length() - 1
     assert groups == 1 << bits
     straight = tuple(range(bits))
-    orders = (straight, straight, straight, straight)
+    turns = (straight, straight[1:2] + straight[:1] + straight[2:], straight[1:] + straight[:1])
+    orders = tuple(turns[piece[3]] for piece in PIECES)
     n_table = time_table.shape[0] + class_table.shape[0]
+    input_turned = jnp.swapaxes(input_weight, 1, 2)
+    bias_turned = bias_weight.T
 
     anywhere = pl.BlockSpec(memory_space=pl.ANY)
     scalars = pl.BlockSpec(memory_space=pltpu.SMEM)
     vmem = pltpu.VMEM
     half_rows = (chains, span, width)
     slots = (4, local, width)
-    messages = 3 * 8 + 6 * 2 + 4 * bits + 3 * (groups - 1) + 5
+    messages = 3 * 8 + 6 * 2 + len(PIECES) * bits + 3 * (groups - 1) + 5
     weights_shape = (4, chunk, width)
     outs = pl.pallas_call(
         functools.partial(layer_kernel, dims, orders),
@@ -943,18 +1010,19 @@
             jax.ShapeDtypeStruct((local, width), BF),
             jax.ShapeDtypeStruct((chains, 4 * heads, queries_local, span), BF),
             jax.ShapeDtypeStruct((groups, 16, width), BF),
-            jax.ShapeDtypeStruct((groups, 16, n_table), BF),
+            jax.ShapeDtypeStruct((time_table.shape[1], 2 * groups * 16), F32),
+            jax.ShapeDtypeStruct((n_table, time_table.shape[1]), F32),
             jax.ShapeDtypeStruct((16, channels), F32),
             jax.ShapeDtypeStruct(weights_shape, F32),
         ),
         in_specs=[scalars] * 3 + [anywhere] * 11,
-        out_specs=[anywhere] * 7,
+        out_specs=[anywhere] * 8,
         scratch_shapes=[
             vmem((local, width), BF),
             vmem((local, width), BF),
             vmem((PAIR_SLOTS, PAIR_ROWS, span, channels), BF),
-            vmem(bias_weight.shape, BF),
-            vmem(input_weight.shape, BF),
+            vmem(bias_turned.shape, BF),
+            vmem(input_turned.shape, BF),
             vmem(output_weight.shape, BF),
             vmem(hidden_weight.shape, BF),
             vmem(down_weight.shape, BF),
@@ -988,8 +1056,6 @@
             vmem((4, 3, local, width), BF),
             vmem((width, rows), BF),
             vmem((width, rows), BF),
-            vmem((4, groups, chunk, width), BF),
-            vmem((4, groups, chunk, width), BF),
             vmem(weights_shape, F32),
             vmem((local, width), F32),
             vmem((local, width), F32),
@@ -1005,12 +1071,15 @@
             vmem((4, 16, channels), F32),
             vmem((groups, 16, channels), F32),
             vmem((16, channels), F32),
+            vmem((time_table.shape[1], 2 * groups * 16), F32),
+            vmem((n_table, time_table.shape[1]), F32),
             pltpu.SemaphoreType.DMA((11,)),
             pltpu.SemaphoreType.DMA((PAIR_SLOTS,)),
-            pltpu.SemaphoreType.DMA((8,)),
+            pltpu.SemaphoreType.DMA((14,)),
             pltpu.SemaphoreType.DMA((messages,)),
             pltpu.SemaphoreType.DMA((messages,)),
-        ],
+        ]
+        + [vmem((groups, chunk, piece[2]), BF) for piece in PIECES] * 2,
         compiler_params=pltpu.CompilerParams(
             collective_id=0, has_side_effects=True, vmem_limit_bytes=VMEM_BYTES
         ),
@@ -1022,8 +1091,8 @@
         tokens,
         cotangent,
         pair_features,
-        bias_weight,
-        input_weight,
+        bias_turned,
+        input_turned,
         output_weight,
         hidden_weight,
         down_weight,
@@ -1031,72 +1100,45 @@
         time_table,
         class_table,
     )
-    result, grad_tokens, scores, mods_all, hots, bias_grad, weights = outs
-
-    blocks = queries_local // PAIR_ROWS
-
-    def whole(shape):
-        return pl.BlockSpec(shape, lambda i: (0,) * len(shape))
-
-    kept = weights
-    sixth = modulation_weight.shape[1] // 6
-
-    def by_vector(i):
-        return (0, jnp.minimum(i, 5))
+    result, grad_tokens, scores, mods_all, expanded, tables, bias_grad, weights = outs
 
     outs = pl.pallas_call(
         functools.partial(finish_kernel, dims),
-        grid=(chains * blocks,),
         out_shape=(
             jax.ShapeDtypeStruct((local, width), BF),
             jax.ShapeDtypeStruct((local, width), BF),
             jax.ShapeDtypeStruct(pair_features.shape, BF),
-            jax.ShapeDtypeStruct(bias_weight.shape, F32),
+            jax.ShapeDtypeStruct(bias_turned.shape, F32),
             jax.ShapeDtypeStruct((3, chunk, local_width), F32),
             jax.ShapeDtypeStruct((local_width, chunk), F32),
             jax.ShapeDtypeStruct((2, chunk, hidden), F32),
-            jax.ShapeDtypeStruct((hidden, chunk), F32),
+            jax.ShapeDtypeStruct((chunk, hidden), F32),
             jax.ShapeDtypeStruct(modulation_weight.shape, F32),
             jax.ShapeDtypeStruct(time_table.shape, F32),
             jax.ShapeDtypeStruct(class_table.shape, F32),
         ),
-        in_specs=[
-            anywhere,
-            anywhere,
-            anywhere,
-            whole(scores.shape),
-            whole(mods_all.shape),
-            whole(hots.shape),
-            whole(bias_grad.shape),
-            pl.BlockSpec((2, chunk, width), lambda i: (0, 0, 0)),
-            whole(bias_weight.shape),
-            pl.BlockSpec((modulation_weight.shape[0], sixth), by_vector),
-            whole(time_table.shape),
-            whole(class_table.shape),
+        in_specs=[anywhere] * 9,
+        out_specs=[anywhere] * 11,
+        scratch_shapes=[
+            vmem((2, local, width), BF),
+            vmem(weights.shape, F32),
+            vmem(scores.shape, BF),
+            vmem(mods_all.shape, BF),
+            vmem(expanded.shape, F32),
+            vmem(tables.shape, F32),
+            vmem(bias_grad.shape, F32),
+            vmem(bias_turned.shape, BF),
+            vmem((PAIR_ROWS, 4 * heads * PAIR_ROWS, channels), BF),
+            vmem((PAIR_SLOTS, PAIR_ROWS, span, channels), BF),
+            vmem((6, modulation_weight.shape[0], width), F32),
+            vmem((3, chunk, local_width), F32),
+            vmem((local_width, chunk), F32),
+            vmem(bias_turned.shape, F32),
+            pltpu.SemaphoreType.DMA((10,)),
+            pltpu.SemaphoreType.DMA((PAIR_SLOTS,)),
+            pltpu.SemaphoreType.DMA((16,)),
         ],
-        out_specs=[
-            anywhere,
-            anywhere,
-            pl.BlockSpec(
-                (None, PAIR_ROWS, span, channels), lambda i: (i // blocks, lax.rem(i, blocks), 0, 0)
-            ),
-            whole(bias_weight.shape),
-            whole((3, chunk, local_width)),
-            whole((local_width, chunk)),
-            anywhere,
-            whole((hidden, chunk)),
-            pl.BlockSpec((modulation_weight.shape[0], sixth), by_vector),
-            whole(time_table.shape),
-            whole(class_table.shape),
-        ],
-        scratch_shapes=[
-            vmem((2, 16 * queries_local, 128), F32),
-            vmem((16, channels), BF),
-            vmem((2, groups * 16, time_table.shape[1]), BF),
-            vmem((groups * 16, time_table.shape[1]), F32),
-            pltpu.SemaphoreType.DMA((4,)),
-        ],
-        compiler_params=pltpu.CompilerParams(vmem_limit_bytes=48 << 20),
+        compiler_params=pltpu.CompilerParams(vmem_limit_bytes=VMEM_BYTES),
         name="finish",
     )(
         result,
@@ -1104,15 +1146,14 @@
         weights,
         scores,
         mods_all,
-        hots,
+        expanded,
+        tables,
         bias_grad,
-        kept,
-        bias_weight,
-        modulation_weight,
-        time_table,
-        class_table,
+        bias_turned,
     )
-    return outs
+    outs = list(outs)
+    outs[3], outs[7] = outs[3].T, outs[7].T
+    return tuple(outs)
 
 
 def solution(mesh):

time: 144 us -> 116 us (0.81); the launches traced: 142 us -> 116 us
  Pallas kernels: 129 us -> 115 us
  local copies, waits for them, and re-layouts: 12 us -> 0 us
    pallas_call x1, Pallas kernels: 117 us -> 105 us  [body(): pl.pallas_call(functools.partial(layer_kernel, dims, orders), out_shape=(...]
    unnamed x24 -> x0, local copies, waits for them, and re-layouts: 10.4 us -> none
    pallas_call x1, Pallas kernels: 12.8 us -> 10.6 us  [body(): pl.pallas_call(functools.partial(finish_kernel, dims), out_shape=(jax.Sha...]
    pallas_call x2 -> x0, local copies, waits for them, and re-layouts: 1.56 us -> none  [body(): pl.pallas_call(functools.partial(finish_kernel, dims), grid=(chains * blo...]
where the time goes in v2:
time: 116 us
  Pallas kernels  115 us (99%)
    pallas_call x1, Pallas kernels, body(): pl.pallas_call(functools.partial(layer_kernel, dims, orders), out_shape=(...  105 us
    pallas_call x1, Pallas kernels, body(): pl.pallas_call(functools.partial(finish_kernel, dims), out_shape=(jax.Sha...  10.6 us

profile of v2, /device:TPU:0, one launch (start us, length us, event | category | flops | bytes accessed | tf_op | source)
XLA Modules:
  0.0 115.9 jit_solution(7913820461859079250)
XLA Ops:
  0.6 104.6 %layer.1 = (bf16[128,768]{1,0:T(8,128)(2,1)}, bf16[128,768]{1,0:T(8,128)(2,1)}, bf16[2,12,64,256]{3,2,1,0:T(8,128)(2,1)}, bf16[8,16,768]{2,1,0:T(8,128)(2,1)}, f...) custom-call(s32[2]{0:T(128)} %length_ref.1, s32[2]{0:T(128)} %time_ref.1, ...), custom_call_target="tpu_custom_call" | custom-call | tf_op jit(solution)/shard_map/layer/pallas_call | solution.py:1006
  105.2 10.6 %finish.1 = (bf16[128,768]{1,0:T(8,128)(2,1)}, bf16[128,768]{1,0:T(8,128)(2,1)}, bf16[2,64,256,256]{3,2,1,0:T(8,128)(2,1)}, f32[12,256]{1,0:T(8,128)}, f32[3,96,...) custom-call(bf16[128,768]{1,0:T(8,128)(2,1)} %get-tuple-element.30.r, ...), custom_call_target="tpu_custom_call" | custom-call | tf_op jit(solution)/shard_map/finish/pallas_call | solution.py:1105

commit v3 on v2

--- a/solution.py
+++ b/solution.py
@@ -14,17 +14,28 @@
 MESH = pl.DeviceIdType.MESH
 PAIR_SLOTS = 4
 PAIR_ROWS = 16
+GATHER_PARTS = 2
 VMEM_BYTES = 60 << 20
 PIECES = (
-    (0, 0, 384, 2),
+    (0, 0, 384, 0),
     (0, 384, 384, 2),
-    (2, 0, 384, 0),
+    (2, 0, 384, 1),
     (2, 384, 384, 0),
     (3, 0, 384, 0),
-    (3, 384, 384, 0),
+    (3, 384, 384, 1),
     (1, 0, 256, 0),
     (1, 256, 256, 0),
     (1, 512, 256, 0),
+)
+SUMS = (
+    (0, 2),
+    (1, 3),
+    (0, 2, 4),
+    (1, 3),
+    (5,),
+    (2, 4, 6, 3),
+    (5, 7, 4, 6, 8),
+    (0, 5, 7, 1, 6, 8, 7, 8),
 )
 
 
@@ -82,22 +93,36 @@
 
 
 class Gather:
-    def __init__(self, remote, slots, here, near, far, near_device, far_device):
-        self.remote, self.slots, self.far, self.near_device = remote, slots, far, near_device
-        self.to_far = remote.start(slots.at[here], slots.at[here], far_device)
-        self.to_near = remote.start(slots.at[here], slots.at[here], near_device)
+    def __init__(self, remote, slots, here, far, near_device, far_device):
+        self.remote, self.slots, self.here, self.far = remote, slots, here, far
+        self.near_device, self.far_device = near_device, far_device
+        self.rows = slots.shape[1] // GATHER_PARTS
+        self.to_far, self.to_near, self.passed = [], [], []
+
+    def view(self, slot, part):
+        return self.slots.at[slot, pl.ds(part * self.rows, self.rows)]
+
+    def start(self, *parts):
+        for part in parts:
+            own = self.view(self.here, part)
+            self.to_far.append(self.remote.start(own, own, self.far_device))
+        for part in parts:
+            own = self.view(self.here, part)
+            self.to_near.append(self.remote.start(own, own, self.near_device))
 
     def forward(self):
-        self.to_far.wait_recv()
-        self.passed = self.remote.start(
-            self.slots.at[self.far], self.slots.at[self.far], self.near_device
-        )
+        for part, copy in enumerate(self.to_far):
+            copy.wait_recv()
+            other = self.view(self.far, part)
+            self.passed.append(self.remote.start(other, other, self.near_device))
 
     def wait_near(self):
-        self.to_near.wait_recv()
+        for copy in self.to_near:
+            copy.wait_recv()
 
     def wait_rest(self):
-        self.passed.wait_recv()
+        for copy in self.passed:
+            copy.wait_recv()
 
 
 class Scatter:
@@ -159,15 +184,21 @@
         self.store[keep] = total.astype(BF)
         self.send()
 
-    def finish(self):
-        while self.step < len(self.order):
-            self.sum()
-        return self.result
+    def done(self):
+        return self.step == len(self.order)
 
 
 def padded(rows):
     more = jnp.zeros((16 - rows.shape[0], rows.shape[1]), F32)
     return jnp.concatenate([rows.astype(F32), more], axis=0).astype(BF)
+
+
+def mod_rows(gathered):
+    half = gathered.shape[3]
+    pieces = [gathered[index].reshape(-1, half) for index in range(4)]
+    return jnp.concatenate(
+        [jnp.concatenate(pieces[2 * chain : 2 * chain + 2], axis=1) for chain in range(2)], axis=0
+    )
 
 
 def slot_of(chunk, order):
@@ -216,6 +247,8 @@
     stage,
     hots,
     mods_all,
+    mods_gather,
+    mod_halves,
     rows_attend,
     rows_hidden,
     rows_down,
@@ -250,9 +283,8 @@
     grad_tokens,
     mod_part,
     mod_near,
-    mod_sum,
-    mod_far,
-    bias_grads,
+    bias_quarters,
+    bias_parts,
     bias_sums,
     bias_grad,
     expanded,
@@ -280,6 +312,9 @@
     def dp_device(index):
         return (index, me)
 
+    def gather(slots):
+        return Gather(remote, slots, me, far, near_device, far_device)
+
     barrier = pltpu.get_barrier_semaphore()
     for device in (near_device, far_device, cross_device):
         pl.semaphore_signal(barrier, inc=1, device_id=device, device_id_type=MESH)
@@ -318,16 +353,24 @@
     pair_copy(0).start()
 
     remote = Remote(send_sems, recv_sems)
+    stores = []
+
+    def store(src, dst):
+        copy = pltpu.make_async_copy(src, dst, store_sems.at[len(stores)])
+        copy.start()
+        stores.append(copy)
 
     n_table = tables.shape[0]
     lane = lax.broadcasted_iota(jnp.int32, (16, n_table), 1)
     row = lax.broadcasted_iota(jnp.int32, (16, n_table), 0)
+    hot_lane = lax.broadcasted_iota(jnp.int32, (8, n_table), 1)
     picked = ((row == 0) & (lane == time_ref[chip])) | (
         (row == 1) & (lane == times + class_ref[chip])
     )
-    time_row = jnp.where(row < 8, time_ref[0], time_ref[1])
-    class_row = jnp.where(row < 8, class_ref[0], class_ref[1])
-    hots[dp] = jnp.where((lane == time_row) | (lane == times + class_row), 1.0, 0.0).astype(BF)
+    for chain in range(chains):
+        hots[dp, chain] = jnp.where(
+            (hot_lane == time_ref[chain]) | (hot_lane == times + class_ref[chain]), 1.0, 0.0
+        )
     load_time.wait()
     load_class.wait()
     condition = nn(jnp.where(picked, 1.0, 0.0).astype(BF), tables[...]).astype(BF)
@@ -355,7 +398,8 @@
     bias_rows = padded(bias_weight[...])
 
     pl.semaphore_wait(barrier, 3 + groups - 1)
-    gather_attend = Gather(remote, rows_attend, me, near, far, near_device, far_device)
+    gather_attend = gather(rows_attend)
+    gather_attend.start(*range(GATHER_PARTS))
     hot_copies = []
     for step in range(1, groups):
         device = dp_device(lax.rem(dp + step, groups))
@@ -405,7 +449,8 @@
             load_down = load(down_hbm, down_weight)
             load_hidden = load(hidden_hbm, hidden_weight)
 
-    gather_down = Gather(remote, rows_down, me, near, far, near_device, far_device)
+    gather_down = gather(rows_down)
+    gather_down.start(*range(GATHER_PARTS // 2))
 
     for index in range(PAIR_SLOTS):
         pair_copy(index).start()
@@ -484,6 +529,7 @@
     bias_copies[1][1].wait_recv()
     bias_copies[0][2].wait_recv()
     scatter_attend.across()
+    gather_down.start(*range(GATHER_PARTS // 2, GATHER_PARTS))
     attend(chip)
     put(part, chip, nn(attended[chip], output_weight[...]))
     scatter_attend.local()
@@ -499,11 +545,6 @@
                 rows[slot * local : (slot + 1) * local]
             )
 
-    gather_down.forward()
-    gather_down.wait_near()
-    back_down(chip)
-    gather_down.wait_rest()
-    back_down(away)
 
     gate_attend = sigmoid(mod(2))
     out_total = scatter_attend.total()
@@ -513,7 +554,13 @@
     normed, inverse_hidden = layer_norm(total)
     norm_hidden[...] = normed
     rows_hidden[me] = (normed * (1.0 + mod(3)) + mod(4)).astype(BF)
-    gather_hidden = Gather(remote, rows_hidden, me, near, far, near_device, far_device)
+    gather_hidden = gather(rows_hidden)
+    gather_hidden.start(*range(GATHER_PARTS))
+    gather_down.forward()
+    gather_down.wait_near()
+    back_down(chip)
+    gather_down.wait_rest()
+    back_down(away)
 
     load_hidden.wait()
 
@@ -563,14 +610,26 @@
 
     sums = {}
 
-    def advance(*indices):
-        for index in indices:
-            sums[index].sum()
-
-    def complete(*indices):
-        for index in indices:
-            matrix, first, size = PIECES[index][:3]
-            final_weights[matrix, :, first : first + size] = sums[index].finish()
+    missing = {matrix: sum(piece[0] == matrix for piece in PIECES) for matrix in range(4)}
+
+    def take_sum(index):
+        matrix, first, size = PIECES[index][:3]
+        sums[index].sum()
+        if sums[index].done():
+            final_weights[matrix, :, first : first + size] = sums[index].result
+            missing[matrix] -= 1
+            if missing[matrix] == 0:
+                store(final_weights.at[matrix], weights_out.at[matrix])
+
+    def advance(place):
+        for index in SUMS[place]:
+            take_sum(index)
+
+    def take_rest():
+        while any(missing.values()):
+            for index in range(len(PIECES)):
+                if not sums[index].done():
+                    take_sum(index)
 
     def flat(ref):
         return ref[...].reshape(chains * span, ref.shape[-1])
@@ -596,8 +655,6 @@
     scatter_down = scatter(2, part_down)
     scatter_down.pre()
 
-    scatter_down.across()
-    scatter_down.local()
     turn_rows(rows_hidden, turned_more)
     weight_grad((2, 3), (turned_more, flat(grad_gate)))
 
@@ -606,7 +663,8 @@
     back = cotangent[...].astype(F32) + norm_back(grad_h * (1.0 + mod(3)), normed, inverse_hidden)
     grad_middle[...] = back
     rows_out[me] = (back * valid * gate_attend).astype(BF)
-    gather_out = Gather(remote, rows_out, me, near, far, near_device, far_device)
+    gather_out = gather(rows_out)
+    gather_out.start(*range(GATHER_PARTS))
 
     weight_grad((4, 5), (turned_more, flat(grad_up)))
 
@@ -617,11 +675,6 @@
     keep_mod(3, grad_h * normed)
     keep_mod(4, grad_h)
     keep_mod(2, back * valid * out_attend[...] * gate_attend * (1.0 - gate_attend))
-    out_total = scatter_down.total()
-    result[...] = (middle[...] + valid * gate_hidden * out_total).astype(BF)
-    keep_mod(
-        5, cotangent[...].astype(F32) * valid * out_total * gate_hidden * (1.0 - gate_hidden)
-    )
     turn_rows(rows_attend, turned)
 
     score_copies = []
@@ -672,7 +725,7 @@
     gather_out.wait_near()
     gather_out.forward()
     back_attend(chip)
-    advance(0, 2)
+    advance(0)
     gather_out.wait_rest()
     back_attend(away)
     scatter_input = scatter(3, part)
@@ -680,15 +733,10 @@
     turn_rows(rows_out, turned_more)
     scatter_input.across()
     scatter_input.local()
+    scatter_down.across()
+    scatter_down.local()
     weight_grad((6, 7, 8), (turned, flat(grad_projected)), (turned_more, flat(attended)))
-    advance(1, 3)
-    stores = []
-
-    def store(src, dst):
-        copy = pltpu.make_async_copy(src, dst, store_sems.at[len(stores)])
-        copy.start()
-        stores.append(copy)
-
+    advance(1)
     for sent in score_copies:
         for copy in sent:
             copy.wait_recv()
@@ -725,12 +773,18 @@
         return lax.fori_loop(turn * blocks, (turn + 1) * blocks, bias_grad_block, total)
 
     total = bias_grad_chain(0, jnp.zeros((16, pair_hbm.shape[3]), F32))
-    advance(0, 2, 4)
-    bias_grads[0] = bias_grad_chain(1, total)
+    advance(2)
+    total = bias_grad_chain(1, total)
+    half = total.shape[1] // 2
+    for quarter in range(4):
+        rows, lanes = quarter // 2 * 8, quarter % 2 * half
+        bias_quarters[quarter] = total[rows : rows + 8, lanes : lanes + half]
+    tensor_devices = ((near, near_device), (far, far_device), (cross, cross_device))
     tensor_copies = [
-        remote.start(bias_grads.at[0], bias_grads.at[1 + index], device)
-        for index, device in enumerate((near_device, far_device, cross_device))
+        remote.start(bias_quarters.at[owner], bias_parts.at[me], device)
+        for owner, device in tensor_devices
     ]
+    bias_parts[me] = bias_quarters[me]
 
     grad_h = scatter_input.total()
     normed = norm_attend[...]
@@ -739,41 +793,54 @@
     ).astype(BF)
     keep_mod(0, grad_h * normed)
     keep_mod(1, grad_h)
+    out_total = scatter_down.total()
+    result[...] = (middle[...] + valid * gate_hidden * out_total).astype(BF)
+    keep_mod(
+        5, cotangent[...].astype(F32) * valid * out_total * gate_hidden * (1.0 - gate_hidden)
+    )
     to_near = remote.start(mod_part, mod_near, near_device)
 
     store(result, result_out)
     store(grad_tokens, grad_tokens_out)
 
-    advance(1, 3)
+    advance(3)
 
     to_near.wait_recv()
-    mod_sum[...] = mod_part[...] + mod_near[...]
-    to_far = remote.start(mod_sum, mod_far, far_device)
+    chain_mods = mod_part[...] + mod_near[...]
+    mod_halves[0] = chain_mods[:, : width // 2].astype(BF)
+    mod_halves[1] = chain_mods[:, width // 2 :].astype(BF)
+    mods_gather[dp] = mod_halves[core]
+    mod_copies = [
+        remote.start(mods_gather.at[dp], mods_gather.at[dp], dp_device(lax.rem(dp + step, groups)))
+        for step in range(1, groups)
+    ]
     for copy in tensor_copies:
         copy.wait_recv()
-    bias_sums[0] = bias_grads[0] + bias_grads[1] + bias_grads[2] + bias_grads[3]
+    bias_sums[0] = bias_parts[0] + bias_parts[1] + bias_parts[2] + bias_parts[3]
     bias_copies = [
         remote.start(bias_sums.at[0], bias_sums.at[step], dp_device(lax.rem(dp + step, groups)))
         for step in range(1, groups)
     ]
+    advance(4)
     advance(5)
-    to_far.wait_recv()
-    own, other = mod_sum[...], mod_far[...]
-    low = jnp.where(chip == 0, own, other)
-    high = jnp.where(chip == 0, other, own)
-    mods_all[dp] = jnp.concatenate([low, high], axis=0).astype(BF)
+    for copy in mod_copies:
+        copy.wait_recv()
+    mods_all[me] = mods_gather[...]
     mod_copies = [
-        remote.start(mods_all.at[dp], mods_all.at[dp], dp_device(lax.rem(dp + step, groups)))
-        for step in range(1, groups)
+        remote.start(mods_gather, mods_all.at[me], device) for _, device in tensor_devices
     ]
-    complete(2)
-    advance(4, 6)
-    complete(3)
-    store(final_weights.at[2], weights_out.at[2])
+    for copy in bias_copies:
+        copy.wait_recv()
+    bias_grad[me] = jnp.sum(bias_sums[...], axis=0)
+    bias_copies = [
+        remote.start(bias_grad.at[me], bias_grad.at[me], device) for _, device in tensor_devices
+    ]
     for copy in hot_copies:
         copy.wait_recv()
-    rows_all = groups * 16
-    hot = hots[...].reshape(rows_all, n_table)
+    rows_all = chains * groups * 8
+    hot = jnp.concatenate(
+        [hots[:, chain].reshape(groups * 8, n_table) for chain in range(chains)], axis=0
+    ).astype(BF)
     hot_lane = lax.broadcasted_iota(jnp.int32, hot.shape, 1)
     zero = jnp.zeros_like(hot)
     time_rows = nn(jnp.where(hot_lane < times, hot, zero), tables[...])
@@ -781,13 +848,11 @@
     expanded[:, :rows_all] = jnp.transpose(time_rows)
     expanded[:, rows_all:] = jnp.transpose(class_rows)
     store(expanded, expanded_out)
-    advance(5, 7)
-    complete(4)
-    advance(6, 8)
+    advance(6)
     for copy in mod_copies:
         copy.wait_recv()
     store(mods_all, mods_out)
-    rows = mods_all[...].reshape(rows_all, width)
+    rows = mod_rows(mods_all)
     member = lax.rem(lax.broadcasted_iota(jnp.int32, (rows_all, 1), 0), 8)
     rest = jnp.zeros((rows_all, tables.shape[1]), F32)
     for vector in range(6):
@@ -800,19 +865,11 @@
         rest = rest - piece.astype(F32)
     tables_grad[...] = table
     store(tables_grad, tables_out)
-    complete(0, 5)
-    store(final_weights.at[3], weights_out.at[3])
-    advance(7)
-    complete(1)
-    store(final_weights.at[0], weights_out.at[0])
     for copy in bias_copies:
         copy.wait_recv()
-    bias_grad[...] = jnp.sum(bias_sums[...], axis=0)
     store(bias_grad, bias_grad_out)
-    complete(6)
-    advance(8)
-    complete(7, 8)
-    store(final_weights.at[1], weights_out.at[1])
+    advance(7)
+    take_rest()
     for copy in stores:
         copy.wait()
     remote.finish()
@@ -870,10 +927,10 @@
 
     moves = (
         (bias_hbm, bias),
+        (expanded_hbm, expanded),
+        (mods_hbm, mods),
         (scores_hbm.at[0], scores.at[0]),
         (scores_hbm.at[1], scores.at[1]),
-        (expanded_hbm, expanded),
-        (mods_hbm, mods),
         (weights_hbm, weights),
         (result_hbm, rows_pass.at[0]),
         (grad_tokens_hbm, rows_pass.at[1]),
@@ -918,25 +975,25 @@
         pair_copy(index).start()
         return carry
 
-    n_blocks = chains * blocks
+    stores = []
+
+    def store(src, dst):
+        stores.append(start(src, dst, store_sems.at[len(stores)]))
+
     loads[1].wait()
     loads[2].wait()
-    lax.fori_loop(0, n_blocks, pair_block, 0)
-
-    stores = []
-
-    def store(src, dst):
-        stores.append(start(src, dst, store_sems.at[len(stores)]))
-
-    loads[3].wait()
-    loads[4].wait()
-    rows = mods[...].reshape(groups * 16, width)
+    rows = mod_rows(mods)
     both = jnp.concatenate([rows, rows], axis=0)
     lane = lax.rem(lax.broadcasted_iota(jnp.int32, expanded.shape, 1), 8)
     for vector in range(6):
         left = jnp.where(lane == vector, expanded[...], 0.0).astype(BF)
         modulation[vector] = nn(left, both)
         store(modulation.at[vector], modulation_out.at[:, pl.ds(vector * width, width)])
+    n_blocks = chains * blocks
+    loads[3].wait()
+    loads[4].wait()
+    lax.fori_loop(0, n_blocks, pair_block, 0)
+
     for copy in loads[5:]:
         copy.wait()
     store(weights.at[0], down_out)
@@ -946,7 +1003,13 @@
     store(rows_pass.at[1], grad_tokens_out)
     store(tables.at[pl.ds(0, times)], time_out)
     store(tables.at[pl.ds(times, class_out.shape[0])], class_out)
-    bias_rows[...] = bias_grad[: 4 * heads]
+    bias_rows[...] = jnp.concatenate(
+        [
+            jnp.concatenate([bias_grad[0], bias_grad[1]], axis=1),
+            jnp.concatenate([bias_grad[2], bias_grad[3]], axis=1),
+        ],
+        axis=0,
+    )[: 4 * heads]
     store(bias_rows, bias_grad_out)
     for index in range(3):
         input_grad[index] = weights[1, :, index * local_width : (index + 1) * local_width]
@@ -1001,7 +1064,7 @@
     vmem = pltpu.VMEM
     half_rows = (chains, span, width)
     slots = (4, local, width)
-    messages = 3 * 8 + 6 * 2 + len(PIECES) * bits + 3 * (groups - 1) + 5
+    messages = 4 * 3 * (1 + GATHER_PARTS) + 6 * 2 + len(PIECES) * bits + 3 * (groups - 1) + 10
     weights_shape = (4, chunk, width)
     outs = pl.pallas_call(
         functools.partial(layer_kernel, dims, orders),
@@ -1009,10 +1072,10 @@
             jax.ShapeDtypeStruct((local, width), BF),
             jax.ShapeDtypeStruct((local, width), BF),
             jax.ShapeDtypeStruct((chains, 4 * heads, queries_local, span), BF),
-            jax.ShapeDtypeStruct((groups, 16, width), BF),
+            jax.ShapeDtypeStruct((4, groups, 8, width // 2), BF),
             jax.ShapeDtypeStruct((time_table.shape[1], 2 * groups * 16), F32),
             jax.ShapeDtypeStruct((n_table, time_table.shape[1]), F32),
-            jax.ShapeDtypeStruct((16, channels), F32),
+            jax.ShapeDtypeStruct((4, 8, channels // 2), F32),
             jax.ShapeDtypeStruct(weights_shape, F32),
         ),
         in_specs=[scalars] * 3 + [anywhere] * 11,
@@ -1030,8 +1093,10 @@
             vmem((n_table, time_table.shape[1]), BF),
             vmem((8, modulation_weight.shape[1]), F32),
             vmem((2, 16 * queries_local, 128), F32),
-            vmem((groups, 16, n_table), BF),
-            vmem((groups, 16, width), BF),
+            vmem((groups, chains, 8, n_table), F32),
+            vmem((4, groups, 8, width // 2), BF),
+            vmem((groups, 8, width // 2), BF),
+            vmem((2, 8, width // 2), BF),
             vmem(slots, BF),
             vmem(slots, BF),
             vmem(slots, BF),
@@ -1066,11 +1131,10 @@
             vmem((local, width), BF),
             vmem((8, width), F32),
             vmem((8, width), F32),
-            vmem((8, width), F32),
-            vmem((8, width), F32),
-            vmem((4, 16, channels), F32),
-            vmem((groups, 16, channels), F32),
-            vmem((16, channels), F32),
+            vmem((4, 8, channels // 2), F32),
+            vmem((4, 8, channels // 2), F32),
+            vmem((groups, 8, channels // 2), F32),
+            vmem((4, 8, channels // 2), F32),
             vmem((time_table.shape[1], 2 * groups * 16), F32),
             vmem((n_table, time_table.shape[1]), F32),
             pltpu.SemaphoreType.DMA((11,)),

time: 116 us -> 106 us (0.914)
  Pallas kernels: 115 us -> 105 us
    pallas_call x1, Pallas kernels: 105 us -> 95.5 us  [body(): pl.pallas_call(functools.partial(layer_kernel, dims, orders), out_shape=(...]
where the time goes in v3:
time: 106 us
  Pallas kernels  105 us (99%)
    pallas_call x1, Pallas kernels, body(): pl.pallas_call(functools.partial(layer_kernel, dims, orders), out_shape=(...  95.5 us
    pallas_call x1, Pallas kernels, body(): pl.pallas_call(functools.partial(finish_kernel, dims), out_shape=(jax.Sha...  9.86 us

profile of v3, /device:TPU:0, one launch (start us, length us, event | category | flops | bytes accessed | tf_op | source)
XLA Modules:
  0.0 106.2 jit_solution(846439621924016125)
XLA Ops:
  0.6 95.5 %layer.1 = (bf16[128,768]{1,0:T(8,128)(2,1)}, bf16[128,768]{1,0:T(8,128)(2,1)}, bf16[2,12,64,256]{3,2,1,0:T(8,128)(2,1)}, bf16[4,8,8,384]{3,2,1,0:T(8,128)(2,1)}...) custom-call(s32[2]{0:T(128)} %length_ref.1, s32[2]{0:T(128)} %time_ref.1, ...), custom_call_target="tpu_custom_call" | custom-call | tf_op jit(solution)/shard_map/layer/pallas_call | solution.py:1069
  96.1 9.9 %finish.1 = (bf16[128,768]{1,0:T(8,128)(2,1)}, bf16[128,768]{1,0:T(8,128)(2,1)}, bf16[2,64,256,256]{3,2,1,0:T(8,128)(2,1)}, f32[12,256]{1,0:T(8,128)}, f32[3,96,...) custom-call(bf16[128,768]{1,0:T(8,128)(2,1)} %get-tuple-element.30.r, ...), custom_call_target="tpu_custom_call" | custom-call | tf_op jit(solution)/shard_map/finish/pallas_call | solution.py:1169

commit v4 on v3

--- a/solution.py
+++ b/solution.py
@@ -28,14 +28,14 @@
     (1, 512, 256, 0),
 )
 SUMS = (
-    (0, 2),
-    (1, 3),
-    (0, 2, 4),
-    (1, 3),
+    (0, 2,),
+    (1, 3, 2,),
+    (0, 4,),
+    (1, 3,),
     (5,),
-    (2, 4, 6, 3),
-    (5, 7, 4, 6, 8),
-    (0, 5, 7, 1, 6, 8, 7, 8),
+    (2, 4, 6, 3,),
+    (5, 7, 4, 6, 8,),
+    (0, 5, 7, 1, 6, 8, 7, 8,),
 )
 
 
@@ -347,7 +347,10 @@
     load_time = load(time_hbm, tables.at[pl.ds(0, times)])
     load_class = load(class_hbm, tables.at[pl.ds(times, class_hbm.shape[0])])
     load_tokens = load(tokens_hbm, tokens)
-    load_modulation = load(modulation_hbm, modulation_weight)
+    first = pl.ds(0, 2 * width)
+    other = pl.ds(2 * width, 4 * width)
+    load_modulation = load(modulation_hbm.at[:, first], modulation_weight.at[:, first])
+    load_more = load(modulation_hbm.at[:, other], modulation_weight.at[:, other])
     load_cotangent = load(cotangent_hbm, cotangent)
     load_bias = load(bias_hbm, bias_weight)
     pair_copy(0).start()
@@ -378,8 +381,12 @@
     for index in range(1, PAIR_SLOTS):
         pair_copy(index).start()
     load_input = load(input_hbm, input_weight)
-    both = nn(condition, modulation_weight[...])
-    mods[...] = jnp.broadcast_to(both[0:1] + both[1:2], mods.shape)
+
+    def modulate(columns):
+        both = nn(condition, modulation_weight[:, columns])
+        mods[:, columns] = jnp.broadcast_to(both[0:1] + both[1:2], (8, both.shape[1]))
+
+    modulate(slice(0, 2 * width))
 
     def mod(index):
         return mods[0:1, index * width : (index + 1) * width]
@@ -391,15 +398,17 @@
     normed, inverse_attend = layer_norm(tokens[...].astype(F32))
     norm_attend[...] = normed
     rows_attend[me] = (normed * (1.0 + mod(0)) + mod(1)).astype(BF)
+    pl.semaphore_wait(barrier, 3 + groups - 1)
+    gather_attend = gather(rows_attend)
+    gather_attend.start(*range(GATHER_PARTS))
+    load_more.wait()
+    modulate(slice(2 * width, 6 * width))
     load_cotangent.wait()
     gate_hidden = sigmoid(mod(5))
     rows_down[me] = (cotangent[...].astype(F32) * valid * gate_hidden).astype(BF)
     load_bias.wait()
     bias_rows = padded(bias_weight[...])
 
-    pl.semaphore_wait(barrier, 3 + groups - 1)
-    gather_attend = gather(rows_attend)
-    gather_attend.start(*range(GATHER_PARTS))
     hot_copies = []
     for step in range(1, groups):
         device = dp_device(lax.rem(dp + step, groups))
@@ -640,9 +649,9 @@
 
     gather_hidden.wait_near()
     transition(chip)
-    gather_hidden.forward()
     back_hidden(chip)
     put(part_down, chip, nn(active[chip], down_weight[...]))
+    gather_hidden.forward()
     gather_hidden.wait_rest()
     transition(away)
     weight_grad((0, 1), (turned, flat(active)))
@@ -723,8 +732,8 @@
         )
 
     gather_out.wait_near()
+    back_attend(chip)
     gather_out.forward()
-    back_attend(chip)
     advance(0)
     gather_out.wait_rest()
     back_attend(away)

time: 106 us -> 106 us (level)
  no operation moved by 1% of the time
where the time goes in v4:
time: 106 us; the launch traced here: 105 us
  Pallas kernels  105 us (99%)
    pallas_call x1, Pallas kernels, body(): pl.pallas_call(functools.partial(layer_kernel, dims, orders), out_shape=(...  94.8 us
    pallas_call x1, Pallas kernels, body(): pl.pallas_call(functools.partial(finish_kernel, dims), out_shape=(jax.Sha...  9.85 us

profile of v4, /device:TPU:0, one launch (start us, length us, event | category | flops | bytes accessed | tf_op | source)
XLA Modules:
  0.0 105.4 jit_solution(6046979469925837201)
XLA Ops:
  0.6 94.8 %layer.1 = (bf16[128,768]{1,0:T(8,128)(2,1)}, bf16[128,768]{1,0:T(8,128)(2,1)}, bf16[2,12,64,256]{3,2,1,0:T(8,128)(2,1)}, bf16[4,8,8,384]{3,2,1,0:T(8,128)(2,1)}...) custom-call(s32[2]{0:T(128)} %length_ref.1, s32[2]{0:T(128)} %time_ref.1, ...), custom_call_target="tpu_custom_call" | custom-call | tf_op jit(solution)/shard_map/layer/pallas_call | solution.py:1078
  95.4 9.9 %finish.1 = (bf16[128,768]{1,0:T(8,128)(2,1)}, bf16[128,768]{1,0:T(8,128)(2,1)}, bf16[2,64,256,256]{3,2,1,0:T(8,128)(2,1)}, f32[12,256]{1,0:T(8,128)}, f32[3,96,...) custom-call(bf16[128,768]{1,0:T(8,128)(2,1)} %get-tuple-element.30.r, ...), custom_call_target="tpu_custom_call" | custom-call | tf_op jit(solution)/shard_map/finish/pallas_call | solution.py:1178

commit v5 on v4

--- a/solution.py
+++ b/solution.py
@@ -1001,8 +1001,7 @@
     n_blocks = chains * blocks
     loads[3].wait()
     loads[4].wait()
-    lax.fori_loop(0, n_blocks, pair_block, 0)
-
+    lax.fori_loop(0, blocks, pair_block, 0)
     for copy in loads[5:]:
         copy.wait()
     store(weights.at[0], down_out)
@@ -1025,6 +1024,8 @@
     store(input_grad, input_out)
     output_grad[...] = jnp.transpose(weights[1, :, 3 * local_width :])
     store(output_grad, output_out)
+    lax.fori_loop(blocks, n_blocks, pair_block, 0)
+
     for index in range(n_blocks - PAIR_SLOTS, n_blocks):
         pair_copy(index).wait()
     for copy in stores:

time: 106 us -> 105 us (level)
  no operation moved by 1% of the time
where the time goes in v5:
time: 105 us
  Pallas kernels  104 us (99%)
    pallas_call x1, Pallas kernels, body(): pl.pallas_call(functools.partial(layer_kernel, dims, orders), out_shape=(...  94.8 us
    pallas_call x1, Pallas kernels, body(): pl.pallas_call(functools.partial(finish_kernel, dims), out_shape=(jax.Sha...  9.59 us

profile of v5, /device:TPU:0, one launch (start us, length us, event | category | flops | bytes accessed | tf_op | source)
XLA Modules:
  0.0 105.2 jit_solution(1944753011961192359)
XLA Ops:
  0.6 94.8 %layer.1 = (bf16[128,768]{1,0:T(8,128)(2,1)}, bf16[128,768]{1,0:T(8,128)(2,1)}, bf16[2,12,64,256]{3,2,1,0:T(8,128)(2,1)}, bf16[4,8,8,384]{3,2,1,0:T(8,128)(2,1)}...) custom-call(s32[2]{0:T(128)} %length_ref.1, s32[2]{0:T(128)} %time_ref.1, ...), custom_call_target="tpu_custom_call" | custom-call | tf_op jit(solution)/shard_map/layer/pallas_call | solution.py:1079
  95.4 9.6 %finish.1 = (bf16[128,768]{1,0:T(8,128)(2,1)}, bf16[128,768]{1,0:T(8,128)(2,1)}, bf16[2,64,256,256]{3,2,1,0:T(8,128)(2,1)}, f32[12,256]{1,0:T(8,128)}, f32[3,96,...) custom-call(bf16[128,768]{1,0:T(8,128)(2,1)} %get-tuple-element.30.r, ...), custom_call_target="tpu_custom_call" | custom-call | tf_op jit(solution)/shard_map/finish/pallas_call | solution.py:1179
